TPU v7x, 512 devices: a whole 4x8x8 slice. The times are simulated.
512 devices in a mesh: row: 16 (over z, core), sector: 32 (over x, y).
Axes of the slice: x: 4, y: 8, z: 8, core: 2. Of those that a mesh axis runs over, the one named last changes fastest.
Arguments:
- boundary_in: float32 [32, 128, 256], P('sector'), may hold values from -6 to 6
- left_transfer: float32 [16, 32, 128, 128], P('row', 'sector'), may hold values from -0.25 to 0.25
- right_transfer: float32 [16, 256, 256], P('row'), may hold values from -0.36 to 0.36
- env_weight: bfloat16 [16, 16, 256, 256], P('row'), may hold values from -50000 to 50000
- ranks: int32 [32], P('sector'), may hold values from 32 to 128, as said below
- routes: int32 [32, 16], P('sector'), may hold values from 0 to 31, all different within a row; in each aligned block of 32 rows (0 to 31, 32 to 63, ...) at most 24 rows name the same one
- owner: int32 [32], replicated, may hold values from 0 to 31, each once
Outputs:
- boundary_out: float32 [16, 32, 128, 256], P('row', 'sector')
- environment: float32 [16, 32, 128, 256], P('row', 'sector')
Inputs may be any that keep to these rules, and one draw needn't show every extreme that they name: `ranks`: at least one sector has rank 128. `routes`: each row names 16 different sectors; no sector is named by more than 24 rows. `owner`: each sector index once.
All inputs are finite; a program needn't handle non-finite values.
Results may differ from a plain program's by a relative error of at most 0.013.
Values may be sent and summed in bfloat16 or wider, within the bound.
No kernel may reach another device: no remote copies, remote signals or barrier semaphores. Data moves between devices by JAX's collectives and lax.ppermute only.
A program may use at most 64 MiB of HBM per device.

v0:
```python
import jax
import jax.numpy as jnp
from jax import lax
from jax.sharding import PartitionSpec as P


def passed_along(value, axis, steps):
    count = lax.axis_size(axis)
    leading, last = (max(0, -steps), min(count, count - steps))
    return lax.ppermute(value, axis, [(source, source + steps) for source in range(leading, last)])


def on_device(boundary_in, left_transfer, right_transfer, env_weight, ranks, routes, owner):
    highest = lax.Precision.HIGHEST
    block_size = boundary_in.shape[1]
    pair_size = boundary_in.shape[2]
    sector_count = owner.shape[0]
    kept_rows = (jnp.arange(block_size) < ranks[0]).astype(jnp.float32)
    initial = boundary_in[0] * kept_rows[:, None]
    unit_block = jnp.eye(block_size, dtype=jnp.float32)
    unit_pairs = jnp.eye(pair_size, dtype=jnp.float32)
    left_op = kept_rows[:, None] * (0.9 * unit_block + left_transfer[0, 0]) * kept_rows[None, :]
    right_op = 0.9 * unit_pairs + right_transfer[0]

    def absorb(matrix):
        inner = jnp.dot(left_op, matrix, precision=highest, preferred_element_type=jnp.float32)
        return jnp.dot(inner, right_op, precision=highest, preferred_element_type=jnp.float32)

    row_position = lax.axis_index("row")

    def advance(turn, carried):
        previous = passed_along(carried, "row", 1)
        previous = jnp.where(row_position == 0, initial, previous)
        return absorb(previous)

    current = lax.fori_loop(0, lax.axis_size("row") - 1, advance, absorb(initial))
    rounded = current.astype(jnp.bfloat16)
    partials = jnp.einsum(
        "ab,jbc->jac", rounded, env_weight[0], preferred_element_type=jnp.float32
    ).astype(jnp.bfloat16)
    sector_ids = jnp.arange(sector_count)
    matches = (routes[0][:, None] == sector_ids[None, :]).astype(jnp.int32)
    target_owner = jnp.sum(matches * owner[None, :], axis=1)
    selector = (target_owner[None, :] == sector_ids[:, None]).astype(jnp.bfloat16)
    owner_terms = jnp.einsum("oj,jac->oac", selector, partials, preferred_element_type=jnp.float32)
    environment = lax.psum_scatter(
        owner_terms.astype(jnp.bfloat16), "sector", scatter_dimension=0, tiled=True
    ).astype(jnp.float32)
    return (current[None, None], environment[None])


def solution(mesh):
    return jax.shard_map(
        on_device,
        mesh=mesh,
        in_specs=(
            P("sector", None, None),
            P("row", "sector", None, None),
            P("row", None, None),
            P("row", None, None, None),
            P("sector"),
            P("sector", None),
            P(),
        ),
        out_specs=(P("row", "sector", None, None), P("row", "sector", None, None)),
        check_vma=False,
    )
```

profile of v0, /device:TPU:16, one launch (start us, length us, event | category | flops | bytes accessed | tf_op | source)
XLA Modules:
  0.0 379.7 jit_solution(13815904256197256881)
XLA Ops:
  8.0 0.9 fusion.17
  9.0 1.0 bitcast_multiply_fusion
  9.9 1.3 fusion.12
  11.2 1.0 bitcast_add_fusion
  12.2 1.2 fusion.34
  13.5 0.9 select_reduce_fusion
  14.3 103.1 %while.12 = (s32[]{:T(128)}, f32[128,256]{1,0:T(8,128)S(1)}, pred[]{:T(512)}, f32[128,256]{1,0:T(8,128)S(1)}, f32[128,128]{1,0:T(8,128)S(1)}, /*index=5*/f32[256,256]{1,0:T(8,128)S(1)}, s32[]{:T(128)}) while((s32[]{:T(128)}, f32[128,256]{1,0:T(8,128)S(1)}, pred[]{:T(512)}, f32[128,256]{1,0:T(8,128)S(1)}, f32[128,128]{1,0:T(8,128)S(1)}, ...), condition=%wide.region_1.2_spmd, body=%wide.region_0.1_spmd.sunk | while | flops 151027712 | bytes 1507446 | solution.py:36
  14.3 1.7 collective-permute-start
  16.1 1.0 collective-permute-done
  17.4 0.4 fusion.51
  17.9 5.5 %collective-permute-start = (f32[128,256]{1,0:T(8,128)S(1)}, f32[128,256]{1,0:T(8,128)S(1)}, u32[]{:S(2)}, u32[]{:S(2)}) collective-permute-start(f32[128,256]{1,0:T(8,128)S(1)} %get-tuple-element.134), channel_id=1, source_target_pairs={{0,32},{32,64},{64,96},{96,128},{128,160},{160,192},{192,224},{224... | collective-permute-start | bytes 393224 | tf_op jit(solution)/shard_map/while/body/eval_jaxpr/ppermute | solution.py:10
  23.4 1.0 collective-permute-done
  24.8 0.4 fusion.51
  25.2 5.3 %collective-permute-start = (f32[128,256]{1,0:T(8,128)S(1)}, f32[128,256]{1,0:T(8,128)S(1)}, u32[]{:S(2)}, u32[]{:S(2)}) collective-permute-start(f32[128,256]{1,0:T(8,128)S(1)} %get-tuple-element.134), channel_id=1, source_target_pairs={{0,32},{32,64},{64,96},{96,128},{128,160},{160,192},{192,224},{224... | collective-permute-start | bytes 393224 | tf_op jit(solution)/shard_map/while/body/eval_jaxpr/ppermute | solution.py:10
  30.5 1.0 collective-permute-done
  32.3 5.3 %collective-permute-start = (f32[128,256]{1,0:T(8,128)S(1)}, f32[128,256]{1,0:T(8,128)S(1)}, u32[]{:S(2)}, u32[]{:S(2)}) collective-permute-start(f32[128,256]{1,0:T(8,128)S(1)} %get-tuple-element.134), channel_id=1, source_target_pairs={{0,32},{32,64},{64,96},{96,128},{128,160},{160,192},{192,224},{224... | collective-permute-start | bytes 393224 | tf_op jit(solution)/shard_map/while/body/eval_jaxpr/ppermute | solution.py:10
  37.6 1.0 collective-permute-done
  38.9 0.4 fusion.51
  39.4 5.3 %collective-permute-start = (f32[128,256]{1,0:T(8,128)S(1)}, f32[128,256]{1,0:T(8,128)S(1)}, u32[]{:S(2)}, u32[]{:S(2)}) collective-permute-start(f32[128,256]{1,0:T(8,128)S(1)} %get-tuple-element.134), channel_id=1, source_target_pairs={{0,32},{32,64},{64,96},{96,128},{128,160},{160,192},{192,224},{224... | collective-permute-start | bytes 393224 | tf_op jit(solution)/shard_map/while/body/eval_jaxpr/ppermute | solution.py:10
  44.7 1.0 collective-permute-done
  46.0 0.4 fusion.51
  46.5 5.3 %collective-permute-start = (f32[128,256]{1,0:T(8,128)S(1)}, f32[128,256]{1,0:T(8,128)S(1)}, u32[]{:S(2)}, u32[]{:S(2)}) collective-permute-start(f32[128,256]{1,0:T(8,128)S(1)} %get-tuple-element.134), channel_id=1, source_target_pairs={{0,32},{32,64},{64,96},{96,128},{128,160},{160,192},{192,224},{224... | collective-permute-start | bytes 393224 | tf_op jit(solution)/shard_map/while/body/eval_jaxpr/ppermute | solution.py:10
  51.8 1.0 collective-permute-done
  53.6 5.3 %collective-permute-start = (f32[128,256]{1,0:T(8,128)S(1)}, f32[128,256]{1,0:T(8,128)S(1)}, u32[]{:S(2)}, u32[]{:S(2)}) collective-permute-start(f32[128,256]{1,0:T(8,128)S(1)} %get-tuple-element.134), channel_id=1, source_target_pairs={{0,32},{32,64},{64,96},{96,128},{128,160},{160,192},{192,224},{224... | collective-permute-start | bytes 393224 | tf_op jit(solution)/shard_map/while/body/eval_jaxpr/ppermute | solution.py:10
  58.9 1.0 collective-permute-done
  60.7 5.3 %collective-permute-start = (f32[128,256]{1,0:T(8,128)S(1)}, f32[128,256]{1,0:T(8,128)S(1)}, u32[]{:S(2)}, u32[]{:S(2)}) collective-permute-start(f32[128,256]{1,0:T(8,128)S(1)} %get-tuple-element.134), channel_id=1, source_target_pairs={{0,32},{32,64},{64,96},{96,128},{128,160},{160,192},{192,224},{224... | collective-permute-start | bytes 393224 | tf_op jit(solution)/shard_map/while/body/eval_jaxpr/ppermute | solution.py:10
  66.0 1.0 collective-permute-done
  67.7 5.3 %collective-permute-start = (f32[128,256]{1,0:T(8,128)S(1)}, f32[128,256]{1,0:T(8,128)S(1)}, u32[]{:S(2)}, u32[]{:S(2)}) collective-permute-start(f32[128,256]{1,0:T(8,128)S(1)} %get-tuple-element.134), channel_id=1, source_target_pairs={{0,32},{32,64},{64,96},{96,128},{128,160},{160,192},{192,224},{224... | collective-permute-start | bytes 393224 | tf_op jit(solution)/shard_map/while/body/eval_jaxpr/ppermute | solution.py:10
  73.1 1.0 collective-permute-done
  74.8 5.3 %collective-permute-start = (f32[128,256]{1,0:T(8,128)S(1)}, f32[128,256]{1,0:T(8,128)S(1)}, u32[]{:S(2)}, u32[]{:S(2)}) collective-permute-start(f32[128,256]{1,0:T(8,128)S(1)} %get-tuple-element.134), channel_id=1, source_target_pairs={{0,32},{32,64},{64,96},{96,128},{128,160},{160,192},{192,224},{224... | collective-permute-start | bytes 393224 | tf_op jit(solution)/shard_map/while/body/eval_jaxpr/ppermute | solution.py:10
  80.2 1.0 collective-permute-done
  81.9 5.3 %collective-permute-start = (f32[128,256]{1,0:T(8,128)S(1)}, f32[128,256]{1,0:T(8,128)S(1)}, u32[]{:S(2)}, u32[]{:S(2)}) collective-permute-start(f32[128,256]{1,0:T(8,128)S(1)} %get-tuple-element.134), channel_id=1, source_target_pairs={{0,32},{32,64},{64,96},{96,128},{128,160},{160,192},{192,224},{224... | collective-permute-start | bytes 393224 | tf_op jit(solution)/shard_map/while/body/eval_jaxpr/ppermute | solution.py:10
  87.3 1.0 collective-permute-done
  88.6 0.4 fusion.51
  89.0 5.3 %collective-permute-start = (f32[128,256]{1,0:T(8,128)S(1)}, f32[128,256]{1,0:T(8,128)S(1)}, u32[]{:S(2)}, u32[]{:S(2)}) collective-permute-start(f32[128,256]{1,0:T(8,128)S(1)} %get-tuple-element.134), channel_id=1, source_target_pairs={{0,32},{32,64},{64,96},{96,128},{128,160},{160,192},{192,224},{224... | collective-permute-start | bytes 393224 | tf_op jit(solution)/shard_map/while/body/eval_jaxpr/ppermute | solution.py:10
  94.4 1.0 collective-permute-done
  96.1 5.3 %collective-permute-start = (f32[128,256]{1,0:T(8,128)S(1)}, f32[128,256]{1,0:T(8,128)S(1)}, u32[]{:S(2)}, u32[]{:S(2)}) collective-permute-start(f32[128,256]{1,0:T(8,128)S(1)} %get-tuple-element.134), channel_id=1, source_target_pairs={{0,32},{32,64},{64,96},{96,128},{128,160},{160,192},{192,224},{224... | collective-permute-start | bytes 393224 | tf_op jit(solution)/shard_map/while/body/eval_jaxpr/ppermute | solution.py:10
  101.5 1.0 collective-permute-done
  103.2 5.3 %collective-permute-start = (f32[128,256]{1,0:T(8,128)S(1)}, f32[128,256]{1,0:T(8,128)S(1)}, u32[]{:S(2)}, u32[]{:S(2)}) collective-permute-start(f32[128,256]{1,0:T(8,128)S(1)} %get-tuple-element.134), channel_id=1, source_target_pairs={{0,32},{32,64},{64,96},{96,128},{128,160},{160,192},{192,224},{224... | collective-permute-start | bytes 393224 | tf_op jit(solution)/shard_map/while/body/eval_jaxpr/ppermute | solution.py:10
  108.6 1.0 collective-permute-done
  110.3 5.3 %collective-permute-start = (f32[128,256]{1,0:T(8,128)S(1)}, f32[128,256]{1,0:T(8,128)S(1)}, u32[]{:S(2)}, u32[]{:S(2)}) collective-permute-start(f32[128,256]{1,0:T(8,128)S(1)} %get-tuple-element.134), channel_id=1, source_target_pairs={{0,32},{32,64},{64,96},{96,128},{128,160},{160,192},{192,224},{224... | collective-permute-start | bytes 393224 | tf_op jit(solution)/shard_map/while/body/eval_jaxpr/ppermute | solution.py:10
  115.7 1.0 collective-permute-done
  117.0 0.4 fusion.51
  117.4 0.4 fusion.8
  117.9 0.9 convolution_convert_fusion
  118.8 2.5 copy.12
  121.4 250.0 %reduce-scatter.2.cloned.1.call-done = bf16[1,128,256]{2,1,0:T(8,128)(2,1)} async-done(((bf16[32,128,256]{2,1,0:T(8,128)(2,1)}), bf16[1,128,256]{2,1,0:T(8,128)(2,1)}) %reduce-scatter.2.cloned.1.call-update) | async-done | bytes 65552 | tf_op jit(solution)/shard_map/reduce_scatter | solution.py:46
  371.4 1.5 bitcast_convert_fusion
  (31 shorter events, 9.4 us)
Async XLA Ops:
  7.2 110.3 %copy-start = (bf16[1,16,256,256]{3,2,1,0:T(8,128)(2,1)S(1)}, bf16[1,16,256,256]{3,2,1,0:T(8,128)(2,1)}, u32[]{:S(2)}) copy-start(bf16[1,16,256,256]{3,2,1,0:T(8,128)(2,1)} %param.12) | copy-start | bytes 6291460
  7.2 364.2 %reduce-scatter.2.cloned.1.call-start = ((), (), s32[]{:S(2)}) async-start(), calls=%async_computation.1 | async-start | bytes 2162688 | tf_op jit(solution)/shard_map/reduce_scatter | solution.py:46
  14.3 2.7 collective-permute-start
  17.9 6.5 %collective-permute-start = (f32[128,256]{1,0:T(8,128)S(1)}, f32[128,256]{1,0:T(8,128)S(1)}, u32[]{:S(2)}, u32[]{:S(2)}) collective-permute-start(f32[128,256]{1,0:T(8,128)S(1)} %get-tuple-element.134), channel_id=1, source_target_pairs={{0,32},{32,64},{64,96},{96,128},{128,160},{160,192},{192,224},{224... | collective-permute-start | bytes 393224 | tf_op jit(solution)/shard_map/while/body/eval_jaxpr/ppermute | solution.py:10
  25.2 6.3 %collective-permute-start = (f32[128,256]{1,0:T(8,128)S(1)}, f32[128,256]{1,0:T(8,128)S(1)}, u32[]{:S(2)}, u32[]{:S(2)}) collective-permute-start(f32[128,256]{1,0:T(8,128)S(1)} %get-tuple-element.134), channel_id=1, source_target_pairs={{0,32},{32,64},{64,96},{96,128},{128,160},{160,192},{192,224},{224... | collective-permute-start | bytes 393224 | tf_op jit(solution)/shard_map/while/body/eval_jaxpr/ppermute | solution.py:10
  32.3 6.3 %collective-permute-start = (f32[128,256]{1,0:T(8,128)S(1)}, f32[128,256]{1,0:T(8,128)S(1)}, u32[]{:S(2)}, u32[]{:S(2)}) collective-permute-start(f32[128,256]{1,0:T(8,128)S(1)} %get-tuple-element.134), channel_id=1, source_target_pairs={{0,32},{32,64},{64,96},{96,128},{128,160},{160,192},{192,224},{224... | collective-permute-start | bytes 393224 | tf_op jit(solution)/shard_map/while/body/eval_jaxpr/ppermute | solution.py:10
  39.4 6.3 %collective-permute-start = (f32[128,256]{1,0:T(8,128)S(1)}, f32[128,256]{1,0:T(8,128)S(1)}, u32[]{:S(2)}, u32[]{:S(2)}) collective-permute-start(f32[128,256]{1,0:T(8,128)S(1)} %get-tuple-element.134), channel_id=1, source_target_pairs={{0,32},{32,64},{64,96},{96,128},{128,160},{160,192},{192,224},{224... | collective-permute-start | bytes 393224 | tf_op jit(solution)/shard_map/while/body/eval_jaxpr/ppermute | solution.py:10
  46.5 6.3 %collective-permute-start = (f32[128,256]{1,0:T(8,128)S(1)}, f32[128,256]{1,0:T(8,128)S(1)}, u32[]{:S(2)}, u32[]{:S(2)}) collective-permute-start(f32[128,256]{1,0:T(8,128)S(1)} %get-tuple-element.134), channel_id=1, source_target_pairs={{0,32},{32,64},{64,96},{96,128},{128,160},{160,192},{192,224},{224... | collective-permute-start | bytes 393224 | tf_op jit(solution)/shard_map/while/body/eval_jaxpr/ppermute | solution.py:10
  53.6 6.3 %collective-permute-start = (f32[128,256]{1,0:T(8,128)S(1)}, f32[128,256]{1,0:T(8,128)S(1)}, u32[]{:S(2)}, u32[]{:S(2)}) collective-permute-start(f32[128,256]{1,0:T(8,128)S(1)} %get-tuple-element.134), channel_id=1, source_target_pairs={{0,32},{32,64},{64,96},{96,128},{128,160},{160,192},{192,224},{224... | collective-permute-start | bytes 393224 | tf_op jit(solution)/shard_map/while/body/eval_jaxpr/ppermute | solution.py:10
  60.7 6.3 %collective-permute-start = (f32[128,256]{1,0:T(8,128)S(1)}, f32[128,256]{1,0:T(8,128)S(1)}, u32[]{:S(2)}, u32[]{:S(2)}) collective-permute-start(f32[128,256]{1,0:T(8,128)S(1)} %get-tuple-element.134), channel_id=1, source_target_pairs={{0,32},{32,64},{64,96},{96,128},{128,160},{160,192},{192,224},{224... | collective-permute-start | bytes 393224 | tf_op jit(solution)/shard_map/while/body/eval_jaxpr/ppermute | solution.py:10
  67.7 6.3 %collective-permute-start = (f32[128,256]{1,0:T(8,128)S(1)}, f32[128,256]{1,0:T(8,128)S(1)}, u32[]{:S(2)}, u32[]{:S(2)}) collective-permute-start(f32[128,256]{1,0:T(8,128)S(1)} %get-tuple-element.134), channel_id=1, source_target_pairs={{0,32},{32,64},{64,96},{96,128},{128,160},{160,192},{192,224},{224... | collective-permute-start | bytes 393224 | tf_op jit(solution)/shard_map/while/body/eval_jaxpr/ppermute | solution.py:10
  74.8 6.3 %collective-permute-start = (f32[128,256]{1,0:T(8,128)S(1)}, f32[128,256]{1,0:T(8,128)S(1)}, u32[]{:S(2)}, u32[]{:S(2)}) collective-permute-start(f32[128,256]{1,0:T(8,128)S(1)} %get-tuple-element.134), channel_id=1, source_target_pairs={{0,32},{32,64},{64,96},{96,128},{128,160},{160,192},{192,224},{224... | collective-permute-start | bytes 393224 | tf_op jit(solution)/shard_map/while/body/eval_jaxpr/ppermute | solution.py:10
  81.9 6.3 %collective-permute-start = (f32[128,256]{1,0:T(8,128)S(1)}, f32[128,256]{1,0:T(8,128)S(1)}, u32[]{:S(2)}, u32[]{:S(2)}) collective-permute-start(f32[128,256]{1,0:T(8,128)S(1)} %get-tuple-element.134), channel_id=1, source_target_pairs={{0,32},{32,64},{64,96},{96,128},{128,160},{160,192},{192,224},{224... | collective-permute-start | bytes 393224 | tf_op jit(solution)/shard_map/while/body/eval_jaxpr/ppermute | solution.py:10
  89.0 6.3 %collective-permute-start = (f32[128,256]{1,0:T(8,128)S(1)}, f32[128,256]{1,0:T(8,128)S(1)}, u32[]{:S(2)}, u32[]{:S(2)}) collective-permute-start(f32[128,256]{1,0:T(8,128)S(1)} %get-tuple-element.134), channel_id=1, source_target_pairs={{0,32},{32,64},{64,96},{96,128},{128,160},{160,192},{192,224},{224... | collective-permute-start | bytes 393224 | tf_op jit(solution)/shard_map/while/body/eval_jaxpr/ppermute | solution.py:10
  96.1 6.3 %collective-permute-start = (f32[128,256]{1,0:T(8,128)S(1)}, f32[128,256]{1,0:T(8,128)S(1)}, u32[]{:S(2)}, u32[]{:S(2)}) collective-permute-start(f32[128,256]{1,0:T(8,128)S(1)} %get-tuple-element.134), channel_id=1, source_target_pairs={{0,32},{32,64},{64,96},{96,128},{128,160},{160,192},{192,224},{224... | collective-permute-start | bytes 393224 | tf_op jit(solution)/shard_map/while/body/eval_jaxpr/ppermute | solution.py:10
  103.2 6.3 %collective-permute-start = (f32[128,256]{1,0:T(8,128)S(1)}, f32[128,256]{1,0:T(8,128)S(1)}, u32[]{:S(2)}, u32[]{:S(2)}) collective-permute-start(f32[128,256]{1,0:T(8,128)S(1)} %get-tuple-element.134), channel_id=1, source_target_pairs={{0,32},{32,64},{64,96},{96,128},{128,160},{160,192},{192,224},{224... | collective-permute-start | bytes 393224 | tf_op jit(solution)/shard_map/while/body/eval_jaxpr/ppermute | solution.py:10
  110.3 6.3 %collective-permute-start = (f32[128,256]{1,0:T(8,128)S(1)}, f32[128,256]{1,0:T(8,128)S(1)}, u32[]{:S(2)}, u32[]{:S(2)}) collective-permute-start(f32[128,256]{1,0:T(8,128)S(1)} %get-tuple-element.134), channel_id=1, source_target_pairs={{0,32},{32,64},{64,96},{96,128},{128,160},{160,192},{192,224},{224... | collective-permute-start | bytes 393224 | tf_op jit(solution)/shard_map/while/body/eval_jaxpr/ppermute | solution.py:10
  117.4 1.4 copy-start.1
Sparse Core Ops, SparseCore 0:
  121.5 249.8 reduce-scatter.1
where the time goes:
time: 380 us
  waiting for transfers between devices  264 us (69%)
  starting transfers between devices  76.5 us (20%)
  matrix products  15.5 us (4%)
  between operations  14.9 us (4%)
  other arithmetic  5.25 us (1%)
    reduce_scatter x1, waiting for transfers between devices, on_device(): lax.psum_scatter(owner_terms.astype(jnp.bfloat16), 'sector', scatter_dime...  250 us
    ppermute x15, starting transfers between devices, passed_along(): lax.ppermute(value, axis, [(source, source + steps) for source in range(l...  76.4 us
    ppermute x15, waiting for transfers between devices, passed_along(): lax.ppermute(value, axis, [(source, source + steps) for source in range(l...  14.4 us
  transfers between devices with their start and end apart: 16, of which 16 were waited for; matrix products, arithmetic and copies ran while one was open for 0% of the time, Pallas kernels for 0%

commit v1 on v0

v1 whole, which is shorter than its diff:
```python
import jax
import jax.numpy as jnp
from jax import lax
from jax.experimental import pallas as pl
from jax.experimental.pallas import tpu as pltpu
from jax.sharding import PartitionSpec as P

ALONG = 8
PAIR = 2
EXTRA = 8
VMEM_GRANT = 8 * 1024 * 1024
HIGHEST = lax.Precision.HIGHEST


def whole(space):
    return pl.BlockSpec(memory_space=space)


def times(a, b):
    return jnp.dot(a, b, precision=HIGHEST, preferred_element_type=jnp.float32)


def absorb(left, block, right):
    return times(times(left, block), right)


def packed(left, right):
    half = left.shape[0] // 2
    return jnp.concatenate([right, jnp.concatenate([left[:half], left[half:]], axis=1)], axis=0)


def unpacked(ref):
    pairs = ref.shape[1]
    size = pairs // 2
    below = ref[pairs:, :]
    return jnp.concatenate([below[:, :size], below[:, size:]], axis=0), ref[:pairs, :]


def store_packed(ref, left, right):
    pairs = ref.shape[1]
    half = left.shape[0] // 2
    ref[:pairs, :] = right
    ref[pairs:, : pairs // 2] = left[:half]
    ref[pairs:, pairs // 2 :] = left[half:]


def on_core(kernel, shapes, *operands, scalar=False):
    spaces = [pltpu.VMEM] * len(operands)
    if scalar:
        spaces[0] = pltpu.SMEM
    moved = sum(4 * operand.size for operand in operands)
    return pl.pallas_call(
        kernel,
        out_shape=shapes,
        in_specs=[whole(space) for space in spaces],
        out_specs=[whole(pltpu.VMEM)] * len(shapes),
        compiler_params=pltpu.CompilerParams(vmem_limit_bytes=VMEM_GRANT),
        cost_estimate=pl.CostEstimate(
            flops=256 * moved, bytes_accessed=2 * moved, transcendentals=0
        ),
    )(*operands)


def like(array):
    return jax.ShapeDtypeStruct(array.shape, jnp.float32)


def operators(rank, initial, own, low):
    def kernel(rank_ref, block_ref, own_ref, low_ref, own_out, two_out, block_out):
        rank = rank_ref[0]

        def whole_of(ref):
            left, right = unpacked(ref)
            rows = lax.broadcasted_iota(jnp.int32, left.shape, 0)
            columns = lax.broadcasted_iota(jnp.int32, left.shape, 1)
            kept = jnp.logical_and(rows < rank, columns < rank)
            left = jnp.where(kept, left + jnp.where(rows == columns, 0.9, 0.0), 0.0)
            rows = lax.broadcasted_iota(jnp.int32, right.shape, 0)
            columns = lax.broadcasted_iota(jnp.int32, right.shape, 1)
            return left, right + jnp.where(rows == columns, 0.9, 0.0)

        left, right = whole_of(own_ref)
        store_packed(own_out, left, right)
        left_low, right_low = whole_of(low_ref)
        left, right = times(left, left_low), times(right_low, right)
        store_packed(two_out, left, right)
        block_out[...] = absorb(left, block_ref[...], right)

    shapes = [like(own), like(own), like(initial)]
    return on_core(kernel, shapes, rank, initial, own, low, scalar=True)


def joined(later, earlier):
    def kernel(later_ref, earlier_ref, out_ref):
        left, right = unpacked(later_ref)
        left_before, right_before = unpacked(earlier_ref)
        store_packed(out_ref, times(left, left_before), times(right_before, right))

    return on_core(kernel, [like(later)], later, earlier)[0]


def taken(operator, block):
    def kernel(operator_ref, block_ref, out_ref):
        left, right = unpacked(operator_ref)
        out_ref[...] = absorb(left, block_ref[...], right)

    return on_core(kernel, [like(block)], operator, block)[0]


def last_rows(copies, operator, block, extra):
    rows, columns = block.shape

    def kernel(operator_ref, block_ref, extra_ref, block_out, outgoing_ref):
        left, right = unpacked(operator_ref)
        own = absorb(left, block_ref[...], right)
        block_out[...] = own
        rounded = own.astype(jnp.bfloat16)
        for index in range(copies):
            outgoing_ref[index, :rows, :] = rounded
            outgoing_ref[index, rows:, :] = extra_ref[...]

    outgoing = jax.ShapeDtypeStruct((copies, rows + EXTRA, columns), jnp.bfloat16)
    return on_core(kernel, [like(block), outgoing], operator, block, extra)


def environment_sums(slots, arrived, weights):
    sources, targets = slots.shape
    slot_count, inner, columns = weights.shape
    rows = arrived.shape[1] - EXTRA

    def kernel(slots_ref, arrived_ref, weights_ref, sums_ref):
        def one_target(target, carried):
            total = jnp.zeros((rows, columns), jnp.float32)
            for source in range(sources):
                slot = slots_ref[source, target]
                block = arrived_ref[source, :rows, :]
                block = jnp.where(slot >= 0, block, jnp.zeros_like(block))
                slot = jnp.minimum(jnp.maximum(slot, 0), slot_count - 1)
                total += jnp.dot(block, weights_ref[slot], preferred_element_type=jnp.float32)
            sums_ref[target] = total.astype(jnp.bfloat16)
            return carried

        lax.fori_loop(0, targets, one_target, 0)

    return pl.pallas_call(
        kernel,
        out_shape=jax.ShapeDtypeStruct((targets, rows, columns), jnp.bfloat16),
        in_specs=[whole(pltpu.SMEM), whole(pltpu.VMEM), whole(pltpu.VMEM)],
        out_specs=whole(pltpu.VMEM),
        compiler_params=pltpu.CompilerParams(vmem_limit_bytes=VMEM_GRANT),
        cost_estimate=pl.CostEstimate(
            flops=2 * sources * targets * rows * inner * columns,
            bytes_accessed=2 * (arrived.size + weights.size + targets * rows * columns),
            transcendentals=0,
        ),
    )(slots, arrived, weights)


def on_device(boundary_in, left_transfer, right_transfer, env_weight, ranks, routes, owner):
    block_size = boundary_in.shape[1]
    row_count = lax.axis_size("row")
    sector_count = lax.axis_size("sector")
    row = lax.axis_index("row")
    sector = lax.axis_index("sector")

    def sent(value, pairs):
        return lax.ppermute(value, "row", pairs)

    kept_rows = (jnp.arange(block_size) < ranks[0]).astype(jnp.float32)
    initial = boundary_in[0] * kept_rows[:, None]
    raw = packed(left_transfer[0, 0], right_transfer[0])
    low = sent(raw, [(r, r + 1) for r in range(0, row_count, 2)])
    own, two, block = operators(ranks, initial, raw, low)
    arrived = sent(block, [(1, 3)])
    half = sent(two, [(r, r + 2) for r in range(5, row_count, 4)])

    source = jnp.where(row == 3, arrived, initial)
    block = taken(two, arrived)
    leaving = block
    four = joined(two, half)
    hops = list(range(3, row_count - 4, 4))
    for last in hops:
        arrived = sent(block, [(last, last + 4)])
        source = jnp.where(row == last + 4, arrived, source)
        if last != hops[-1]:
            block = taken(four, arrived)
            leaving = jnp.where(row == last + 4, block, leaving)

    arrived = sent(leaving, [(r, r + 2) for r in range(3, row_count - 2, 4)])
    to_first = [(r + 1, r) for r in range(2, row_count, 2)]
    relayed = sent(half, to_first[2::2])
    source = jnp.where((row % 4 == 1) & (row > 1), arrived, source)
    arrived = sent(source, to_first)
    source = jnp.where((row % 2 == 0) & (row > 0), arrived, source)
    second = row % 2 == 1
    base = jnp.where(second, two, own)
    final = joined(base, jnp.where(second, half, relayed))
    final = jnp.where((row % 4 >= 2) & (row >= 4), final, base)

    along = ALONG
    across = sector_count // along
    parts = along // PAIR
    tiles = [
        [x * along + part * PAIR + y for x in range(across) for y in range(PAIR)]
        for part in range(parts)
    ]
    lines = [
        [x * along + part * PAIR + y for part in range(parts)]
        for x in range(across)
        for y in range(PAIR)
    ]
    sector_ids = jnp.arange(sector_count)
    matches = (routes[0][:, None] == sector_ids[None, :]).astype(jnp.int32)
    target_owner = jnp.sum(matches * owner[None, :], axis=1)
    hits = (target_owner[:, None] == jnp.arange(block_size * 2)[None, :]).astype(jnp.int32)
    slot_of = jnp.sum(hits * (jnp.arange(routes.shape[1]) + 1)[:, None], axis=0)
    extra = jnp.broadcast_to(slot_of.astype(jnp.bfloat16), (EXTRA, block_size * 2))
    current, outgoing = last_rows(across * PAIR, final, source, extra)
    arrived = lax.all_to_all(
        outgoing,
        "sector", 0, 0, axis_index_groups=tiles, tiled=True,
    )
    targets = (sector // along) * along + sector % PAIR + jnp.arange(parts) * PAIR
    wanted = (jnp.arange(block_size * 2)[None, :] == targets[:, None]).astype(jnp.float32)
    slots = jnp.sum(arrived[:, block_size, None, :].astype(jnp.float32) * wanted[None], axis=2)
    sums = environment_sums(slots.astype(jnp.int32) - 1, arrived, env_weight[0])
    terms = lax.all_to_all(sums, "sector", 0, 0, axis_index_groups=lines, tiled=True)
    environment = jnp.sum(terms.astype(jnp.float32), axis=0)
    return (current[None, None], environment[None, None])


def solution(mesh):
    return jax.shard_map(
        on_device,
        mesh=mesh,
        in_specs=(
            P("sector", None, None),
            P("row", "sector", None, None),
            P("row", None, None),
            P("row", None, None, None),
            P("sector"),
            P("sector", None),
            P(),
        ),
        out_specs=(P("row", "sector", None, None), P("row", "sector", None, None)),
        check_vma=False,
    )
```

time: 380 us -> 68.3 us (0.18)
  the two profiles are of different devices: /device:TPU:16 before, /device:TPU:384 now
where the time goes in v1:
time: 68.3 us; the launch traced here: 67.8 us
  waiting for transfers between devices  25.8 us (38%)
  blocking collectives  15.8 us (23%)
  starting transfers between devices  13.2 us (19%)
  Pallas kernels  7.1 us (10%)
  other arithmetic  3.4 us (5%)
  between operations  1.64 us (2%)
  local copies, waits for them, and re-layouts  0.91 us (1%)
    all_to_all x1, blocking collectives, on_device(): lax.all_to_all(sums, 'sector', 0, 0, axis_index_groups=lines, tiled=True)  15.8 us
    ppermute x9, waiting for transfers between devices, sent(): return lax.ppermute(value, 'row', pairs)  15.1 us
    all_to_all x1, waiting for transfers between devices, on_device(): lax.all_to_all(outgoing, 'sector', 0, 0, axis_index_groups=tiles, tiled=T...  10.7 us
    ppermute x9, starting transfers between devices, sent(): return lax.ppermute(value, 'row', pairs)  7.89 us
    all_to_all x1, starting transfers between devices, on_device(): lax.all_to_all(outgoing, 'sector', 0, 0, axis_index_groups=tiles, tiled=T...  5.31 us
    pallas_call x7, Pallas kernels, on_core(): pl.pallas_call(kernel, out_shape=shapes, in_specs=[whole(space) for space...  5.24 us
    pallas_call x1, Pallas kernels, environment_sums(): pl.pallas_call(kernel, out_shape=jax.ShapeDtypeStruct((targets, rows, col...  1.86 us
  transfers between devices with their start and end apart: 10, of which 2 were waited for; matrix products, arithmetic and copies ran while one was open for 2% of the time, Pallas kernels for 3%

profile of v1, /device:TPU:384, one launch (start us, length us, event | category | flops | bytes accessed | tf_op | source)
XLA Modules:
  0.0 67.8 jit_solution(2191328877214281337)
XLA Ops:
  0.6 0.0 copy-start.2
  0.6 0.0 copy-start.3
  0.7 0.8 %slice_bitcast_fusion.1 = (f32[64,128]{1,0:T(8,128)S(1)}, f32[64,128]{1,0:T(8,128)S(1)}) fusion(f32[1,1,128,128]{3,2,1,0:T(8,128)} %param.8), kind=kLoop, calls=%fused_computation.11 | loop fusion | bytes 131072 | tf_op jit(solution)/shard_map/slice | solution.py:29
  1.4 1.0 %maximum_maximum_fusion.own_ref = f32[320,256]{1,0:T(8,128)S(1)} fusion(f32[64,128]{1,0:T(8,128)S(1)} %get-tuple-element.13, f32[64,128]{1,0:T(8,128)S(1)} %get-tuple-element.12, f32[256,256]{1,0:T(8,128)} %bitcast.19), kind=kLoop, calls=%fused_computation.1 | loop fusion | flops 163840 | bytes 655360 | tf_op jit(solution)/shard_map/concatenate | solution.py:29
  2.4 1.8 %collective-permute-start = (f32[320,256]{1,0:T(8,128)S(1)}, f32[320,256]{1,0:T(8,128)S(1)}, u32[]{:S(2)}, u32[]{:S(2)}) collective-permute-start(f32[320,256]{1,0:T(8,128)S(1)} %maximum_maximum_fusion.own_ref), channel_id=1, source_target_pairs={{0,32},{64,96},{128,160},{192,224},{256,288},{320,352},{384,416},{... | collective-permute-start | bytes 983048 | tf_op jit(solution)/shard_map/ppermute | solution.py:167
  4.8 1.0 %bitcast_multiply_fusion.block_ref = f32[128,256]{1,0:T(8,128)S(1)} fusion(f32[1,128,256]{2,1,0:T(8,128)} %param.7, f32[128]{0:T(128)S(1)} %compare_convert_fusion), kind=kLoop, calls=%fused_computation.5 | loop fusion | flops 32768 | bytes 262656 | tf_op jit(solution)/shard_map/mul | solution.py:170
  5.8 0.0 collective-permute-done.low_ref
  5.8 1.0 %shard_map.86 = (f32[320,256]{1,0:T(8,128)S(1)}, f32[320,256]{1,0:T(8,128)S(1)}, f32[128,256]{1,0:T(8,128)S(1)}) custom-call(s32[1]{0:T(128)} %copy.13.rank_ref, f32[128,256]{1,0:T(8,128)S(1)} %bitcast_multiply_fusion.block_ref, f32[320,256]{1,0:T(8,128)S(1)} %maximum_maximum_fusion.own_ref, f32[320,256]{1,0:T(8,128)S(1)} %collective-permute-done.low_ref), custom_call_target="tpu_custom_call" | custom-call | flops 201327616 | bytes 1572872 | tf_op jit(solution)/shard_map/pallas_call | solution.py:52
  6.8 0.7 %collective-permute-start.1 = (f32[320,256]{1,0:T(8,128)S(1)}, f32[320,256]{1,0:T(8,128)S(1)}, u32[]{:S(2)}, u32[]{:S(2)}) collective-permute-start(f32[320,256]{1,0:T(8,128)S(1)} %get-tuple-element.7.later_ref.operator_ref), channel_id=1, source_target_pairs={{160,224},{288,352},{416,480},{161,225},{289,353},{417,481},{162,2... | collective-permute-start | bytes 983048 | tf_op jit(solution)/shard_map/ppermute | solution.py:167
  7.5 0.0 copy-start.1
  7.5 0.8 %collective-permute-start.3 = (f32[128,256]{1,0:T(8,128)S(1)}, f32[128,256]{1,0:T(8,128)S(1)}, u32[]{:S(2)}, u32[]{:S(2)}) collective-permute-start(f32[128,256]{1,0:T(8,128)S(1)} %get-tuple-element.9), channel_id=1, source_target_pairs={{32,96},{33,97},{34,98},{35,99},{36,100},{37,101},{38,102},{39,103... | collective-permute-start | bytes 393224 | tf_op jit(solution)/shard_map/ppermute | solution.py:167
  8.3 0.0 collective-permute-done.3.block_ref
  8.4 0.6 shard_map.89
  9.0 0.7 collective-permute-start.4
  9.7 0.0 copy-done.2
  9.7 0.0 copy-done.3
  9.7 0.2 select_reduce_fusion.1
  9.9 0.0 collective-permute-done.1.earlier_ref
  9.9 0.5 shard_map.88.operator_ref
  10.3 0.0 collective-permute-done.4.block_ref
  10.3 0.6 shard_map.90
  11.0 0.7 collective-permute-start.5
  11.7 0.1 select_reduce_fusion
  11.8 0.7 %collective-permute-start.2 = (f32[320,256]{1,0:T(8,128)S(1)}, f32[320,256]{1,0:T(8,128)S(1)}, u32[]{:S(2)}, u32[]{:S(2)}) collective-permute-start(f32[320,256]{1,0:T(8,128)S(1)} %collective-permute-done.1.earlier_ref), channel_id=1, source_target_pairs={{224,192},{352,320},{480,448},{225,193},{353,321},{481,449},{226,1... | collective-permute-start | bytes 983048 | tf_op jit(solution)/shard_map/ppermute | solution.py:167
  12.5 0.0 collective-permute-done.5.block_ref
  12.5 0.6 shard_map.91
  13.1 0.7 collective-permute-start.7
  13.8 0.7 collective-permute-start.6
  14.6 0.0 collective-permute-done.6
  14.6 0.0 collective-permute-done.7
  14.6 0.0 copy-done.1
  14.6 0.1 select_select_fusion
  14.7 1.3 %collective-permute-start.8 = (f32[128,256]{1,0:T(8,128)S(1)}, f32[128,256]{1,0:T(8,128)S(1)}, u32[]{:S(2)}, u32[]{:S(2)}) collective-permute-start(f32[128,256]{1,0:T(8,128)S(1)} %select_select_fusion), channel_id=1, source_target_pairs={{96,64},{160,128},{224,192},{288,256},{352,320},{416,384},{480,448... | collective-permute-start | bytes 393224 | tf_op jit(solution)/shard_map/ppermute | solution.py:167
  16.0 0.0 collective-permute-done.2
  16.1 0.0 copy-start
  16.1 0.5 shard_map.87
  16.6 15.1 %collective-permute-done.8 = f32[128,256]{1,0:T(8,128)S(1)} collective-permute-done((f32[128,256]{1,0:T(8,128)S(1)}, f32[128,256]{1,0:T(8,128)S(1)}, u32[]{:S(2)}, u32[]{:S(2)}) %collective-permute-start.8) | collective-permute-done | bytes 131104 | tf_op jit(solution)/shard_map/ppermute | solution.py:167
  31.7 1.5 %shard_map.92 = (f32[128,256]{1,0:T(8,128)}, bf16[8,136,256]{2,1,0:T(8,128)(2,1)}) custom-call(f32[320,256]{1,0:T(8,128)S(1)} %broadcast_select_fusion.2.operator_ref, f32[128,256]{1,0:T(8,128)S(1)} %broadcast_select_fusion.3.block_ref, bf16[8,256]{1,0:T(8,128)(2,1)S(1)} %broadcast_in_dim.6.extra_ref), custom_call_target="tpu_custom_call" | custom-call | flops 119537664 | bytes 933888 | tf_op jit(solution)/shard_map/pallas_call | solution.py:52
  33.2 5.3 %all-to-all-start = ((bf16[8,136,256]{2,1,0:T(8,128)(2,1)}), bf16[8,136,256]{2,1,0:T(8,128)(2,1)S(1)}, u32[]{:S(2)}, u32[]{:S(2)}) async-start(bf16[8,136,256]{2,1,0:T(8,128)(2,1)} %get-tuple-element.11), calls=%async_computation | async-start | bytes 1114112 | tf_op jit(solution)/shard_map/all_to_all | solution.py:219
  38.5 0.1 fusion
  38.6 10.7 %all-to-all-done.arrived_ref = bf16[8,136,256]{2,1,0:T(8,128)(2,1)S(1)} async-done(((bf16[8,136,256]{2,1,0:T(8,128)(2,1)}), bf16[8,136,256]{2,1,0:T(8,128)(2,1)S(1)}, u32[]{:S(2)}, u32[]{:S(2)}) %all-to-all-start) | async-done | bytes 557088 | tf_op jit(solution)/shard_map/all_to_all | solution.py:219
  49.3 0.1 multiply_reduce_fusion
  49.4 0.1 copy.9
  49.4 0.0 copy-done
  49.5 1.9 %shard_map.93 = bf16[4,128,256]{2,1,0:T(8,128)(2,1)S(1)} custom-call(s32[8,4]{1,0:T(8,128)S(1)} %convert_add_fusion.slots_ref, bf16[8,136,256]{2,1,0:T(8,128)(2,1)S(1)} %all-to-all-done.arrived_ref, bf16[16,256,256]{2,1,0:T(8,128)(2,1)S(1)} %bitcast.18), custom_call_target="tpu_custom_call" | custom-call | flops 536870912 | bytes 2916352 | tf_op jit(solution)/shard_map/pallas_call | solution.py:145
  51.3 15.8 %all_to_all.10 = bf16[4,128,256]{2,1,0:T(8,128)(2,1)S(1)} all-to-all(bf16[4,128,256]{2,1,0:T(8,128)(2,1)S(1)} %shard_map.93), channel_id=1, replica_groups={{0,2,4,6},{1,3,5,7},{8,10,12,14},{9,11,13,15},{16,18,20,22},{17,19,21,2..., dimensions={0} | all-to-all | bytes 524288 | tf_op jit(solution)/shard_map/all_to_all | solution.py:227
  67.1 0.7 %convert_reduce_fusion = f32[128,256]{1,0:T(8,128)} fusion(bf16[4,128,256]{2,1,0:T(8,128)(2,1)S(1)} %all_to_all.10), kind=kLoop, calls=%fused_computation | loop fusion | flops 229376 | bytes 393216 | tf_op jit(solution)/shard_map/reduce_sum | solution.py:228
  (13 shorter events, 0.2 us)
Async XLA Ops:
  0.6 9.0 %copy-start.2 = (s32[32]{0:T(128)S(1)}, s32[32]{0:T(128)}, u32[]{:S(2)}) copy-start(s32[32]{0:T(128)} %param.13) | copy-start | bytes 388
  0.6 9.0 %copy-start.3 = (s32[1,16]{1,0:T(1,128)S(1)}, s32[1,16]{1,0:T(1,128)}, u32[]{:S(2)}) copy-start(s32[1,16]{1,0:T(1,128)} %param.12) | copy-start | bytes 196
  2.4 3.4 %collective-permute-start = (f32[320,256]{1,0:T(8,128)S(1)}, f32[320,256]{1,0:T(8,128)S(1)}, u32[]{:S(2)}, u32[]{:S(2)}) collective-permute-start(f32[320,256]{1,0:T(8,128)S(1)} %maximum_maximum_fusion.own_ref), channel_id=1, source_target_pairs={{0,32},{64,96},{128,160},{192,224},{256,288},{320,352},{384,416},{... | collective-permute-start | bytes 983048 | tf_op jit(solution)/shard_map/ppermute | solution.py:167
  6.8 3.0 %collective-permute-start.1 = (f32[320,256]{1,0:T(8,128)S(1)}, f32[320,256]{1,0:T(8,128)S(1)}, u32[]{:S(2)}, u32[]{:S(2)}) collective-permute-start(f32[320,256]{1,0:T(8,128)S(1)} %get-tuple-element.7.later_ref.operator_ref), channel_id=1, source_target_pairs={{160,224},{288,352},{416,480},{161,225},{289,353},{417,481},{162,2... | collective-permute-start | bytes 983048 | tf_op jit(solution)/shard_map/ppermute | solution.py:167
  7.5 7.1 %copy-start.1 = (f32[1,128,256]{2,1,0:T(8,128)S(1)}, f32[1,128,256]{2,1,0:T(8,128)}, u32[]{:S(2)}) copy-start(f32[1,128,256]{2,1,0:T(8,128)} %param.7) | copy-start | bytes 393220
  7.5 0.8 %collective-permute-start.3 = (f32[128,256]{1,0:T(8,128)S(1)}, f32[128,256]{1,0:T(8,128)S(1)}, u32[]{:S(2)}, u32[]{:S(2)}) collective-permute-start(f32[128,256]{1,0:T(8,128)S(1)} %get-tuple-element.9), channel_id=1, source_target_pairs={{32,96},{33,97},{34,98},{35,99},{36,100},{37,101},{38,102},{39,103... | collective-permute-start | bytes 393224 | tf_op jit(solution)/shard_map/ppermute | solution.py:167
  9.0 1.3 %collective-permute-start.4 = (f32[128,256]{1,0:T(8,128)S(1)}, f32[128,256]{1,0:T(8,128)S(1)}, u32[]{:S(2)}, u32[]{:S(2)}) collective-permute-start(f32[128,256]{1,0:T(8,128)S(1)} %shard_map.89), channel_id=1, source_target_pairs={{96,224},{97,225},{98,226},{99,227},{100,228},{101,229},{102,230},... | collective-permute-start | bytes 393224 | tf_op jit(solution)/shard_map/ppermute | solution.py:167
  11.0 1.5 %collective-permute-start.5 = (f32[128,256]{1,0:T(8,128)S(1)}, f32[128,256]{1,0:T(8,128)S(1)}, u32[]{:S(2)}, u32[]{:S(2)}) collective-permute-start(f32[128,256]{1,0:T(8,128)S(1)} %shard_map.90), channel_id=1, source_target_pairs={{224,352},{225,353},{226,354},{227,355},{228,356},{229,357},{230,3... | collective-permute-start | bytes 393224 | tf_op jit(solution)/shard_map/ppermute | solution.py:167
  11.8 4.2 %collective-permute-start.2 = (f32[320,256]{1,0:T(8,128)S(1)}, f32[320,256]{1,0:T(8,128)S(1)}, u32[]{:S(2)}, u32[]{:S(2)}) collective-permute-start(f32[320,256]{1,0:T(8,128)S(1)} %collective-permute-done.1.earlier_ref), channel_id=1, source_target_pairs={{224,192},{352,320},{480,448},{225,193},{353,321},{481,449},{226,1... | collective-permute-start | bytes 983048 | tf_op jit(solution)/shard_map/ppermute | solution.py:167
  13.1 1.5 %collective-permute-start.7 = (f32[128,256]{1,0:T(8,128)S(1)}, f32[128,256]{1,0:T(8,128)S(1)}, u32[]{:S(2)}, u32[]{:S(2)}) collective-permute-start(f32[128,256]{1,0:T(8,128)S(1)} %shard_map.91), channel_id=1, source_target_pairs={{352,480},{353,481},{354,482},{355,483},{356,484},{357,485},{358,4... | collective-permute-start | bytes 393224 | tf_op jit(solution)/shard_map/ppermute | solution.py:167
  13.8 0.7 %collective-permute-start.6 = (f32[128,256]{1,0:T(8,128)S(1)}, f32[128,256]{1,0:T(8,128)S(1)}, u32[]{:S(2)}, u32[]{:S(2)}) collective-permute-start(f32[128,256]{1,0:T(8,128)S(1)} %select_select_fusion.1), channel_id=1, source_target_pairs={{96,160},{224,288},{352,416},{97,161},{225,289},{353,417},{98,162}... | collective-permute-start | bytes 393224 | tf_op jit(solution)/shard_map/ppermute | solution.py:167
  14.7 17.0 %collective-permute-start.8 = (f32[128,256]{1,0:T(8,128)S(1)}, f32[128,256]{1,0:T(8,128)S(1)}, u32[]{:S(2)}, u32[]{:S(2)}) collective-permute-start(f32[128,256]{1,0:T(8,128)S(1)} %select_select_fusion), channel_id=1, source_target_pairs={{96,64},{160,128},{224,192},{288,256},{352,320},{416,384},{480,448... | collective-permute-start | bytes 393224 | tf_op jit(solution)/shard_map/ppermute | solution.py:167
  16.1 33.4 %copy-start = (bf16[1,16,256,256]{3,2,1,0:T(8,128)(2,1)S(1)}, bf16[1,16,256,256]{3,2,1,0:T(8,128)(2,1)}, u32[]{:S(2)}) copy-start(bf16[1,16,256,256]{3,2,1,0:T(8,128)(2,1)} %param.10) | copy-start | bytes 6291460
  33.2 16.1 %all-to-all-start = ((bf16[8,136,256]{2,1,0:T(8,128)(2,1)}), bf16[8,136,256]{2,1,0:T(8,128)(2,1)S(1)}, u32[]{:S(2)}, u32[]{:S(2)}) async-start(bf16[8,136,256]{2,1,0:T(8,128)(2,1)} %get-tuple-element.11), calls=%async_computation | async-start | bytes 1114112 | tf_op jit(solution)/shard_map/all_to_all | solution.py:219

commit v2 on v1

--- a/solution.py
+++ b/solution.py
@@ -9,7 +9,6 @@
 PAIR = 2
 EXTRA = 8
 VMEM_GRANT = 8 * 1024 * 1024
-HIGHEST = lax.Precision.HIGHEST
 
 
 def whole(space):
@@ -17,16 +16,19 @@
 
 
 def times(a, b):
-    return jnp.dot(a, b, precision=HIGHEST, preferred_element_type=jnp.float32)
+    def parts(value):
+        head = value.astype(jnp.bfloat16)
+        return head, (value - head.astype(jnp.float32)).astype(jnp.bfloat16)
+
+    def dot(first, second):
+        return jnp.dot(first, second, preferred_element_type=jnp.float32)
+
+    (a_head, a_rest), (b_head, b_rest) = parts(a), parts(b)
+    return dot(a_head, b_head) + (dot(a_head, b_rest) + dot(a_rest, b_head))
 
 
 def absorb(left, block, right):
     return times(times(left, block), right)
-
-
-def packed(left, right):
-    half = left.shape[0] // 2
-    return jnp.concatenate([right, jnp.concatenate([left[:half], left[half:]], axis=1)], axis=0)
 
 
 def unpacked(ref):
@@ -65,29 +67,34 @@
     return jax.ShapeDtypeStruct(array.shape, jnp.float32)
 
 
-def operators(rank, initial, own, low):
-    def kernel(rank_ref, block_ref, own_ref, low_ref, own_out, two_out, block_out):
+def operators(rank, stacked, left_low, right_low):
+    size, pairs = left_low.shape[0], right_low.shape[0]
+
+    def kernel(rank_ref, stacked_ref, left_low_ref, right_low_ref, *outs):
+        own_out, two_out, kept_out, block_out = outs
         rank = rank_ref[0]
-
-        def whole_of(ref):
-            left, right = unpacked(ref)
-            rows = lax.broadcasted_iota(jnp.int32, left.shape, 0)
-            columns = lax.broadcasted_iota(jnp.int32, left.shape, 1)
-            kept = jnp.logical_and(rows < rank, columns < rank)
-            left = jnp.where(kept, left + jnp.where(rows == columns, 0.9, 0.0), 0.0)
-            rows = lax.broadcasted_iota(jnp.int32, right.shape, 0)
-            columns = lax.broadcasted_iota(jnp.int32, right.shape, 1)
-            return left, right + jnp.where(rows == columns, 0.9, 0.0)
-
-        left, right = whole_of(own_ref)
+        rows = lax.broadcasted_iota(jnp.int32, (size, size), 0)
+        columns = lax.broadcasted_iota(jnp.int32, (size, size), 1)
+        kept = jnp.logical_and(rows < rank, columns < rank)
+        unit = jnp.where(rows == columns, 0.9, 0.0).astype(jnp.float32)
+        left = jnp.where(kept, unit + stacked_ref[size + pairs :, :size], 0.0)
+        left_before = jnp.where(kept, unit + left_low_ref[...], 0.0)
+        rows = lax.broadcasted_iota(jnp.int32, (pairs, pairs), 0)
+        columns = lax.broadcasted_iota(jnp.int32, (pairs, pairs), 1)
+        unit = jnp.where(rows == columns, 0.9, 0.0).astype(jnp.float32)
+        right = unit + stacked_ref[size : size + pairs, :]
         store_packed(own_out, left, right)
-        left_low, right_low = whole_of(low_ref)
-        left, right = times(left, left_low), times(right_low, right)
+        left, right = times(left, left_before), times(unit + right_low_ref[...], right)
         store_packed(two_out, left, right)
-        block_out[...] = absorb(left, block_ref[...], right)
-
-    shapes = [like(own), like(own), like(initial)]
-    return on_core(kernel, shapes, rank, initial, own, low, scalar=True)
+        rows = lax.broadcasted_iota(jnp.int32, (size, pairs), 0)
+        kept = jnp.where(rows < rank, stacked_ref[:size, :], 0.0)
+        kept_out[...] = kept
+        block_out[...] = absorb(left, kept, right)
+
+    packed = jax.ShapeDtypeStruct((pairs + size // 2, pairs), jnp.float32)
+    block = jax.ShapeDtypeStruct((size, pairs), jnp.float32)
+    operands = rank, stacked, left_low, right_low
+    return on_core(kernel, [packed, packed, block, block], *operands, scalar=True)
 
 
 def joined(later, earlier):
@@ -99,12 +106,14 @@
     return on_core(kernel, [like(later)], later, earlier)[0]
 
 
-def taken(operator, block):
-    def kernel(operator_ref, block_ref, out_ref):
+def taken(operator, block, copies=1):
+    def kernel(operator_ref, block_ref, *outs):
         left, right = unpacked(operator_ref)
-        out_ref[...] = absorb(left, block_ref[...], right)
-
-    return on_core(kernel, [like(block)], operator, block)[0]
+        result = absorb(left, block_ref[...], right)
+        for out_ref in outs:
+            out_ref[...] = result
+
+    return on_core(kernel, [like(block)] * copies, operator, block)
 
 
 def last_rows(copies, operator, block, extra):
@@ -166,32 +175,40 @@
     def sent(value, pairs):
         return lax.ppermute(value, "row", pairs)
 
-    kept_rows = (jnp.arange(block_size) < ranks[0]).astype(jnp.float32)
-    initial = boundary_in[0] * kept_rows[:, None]
-    raw = packed(left_transfer[0, 0], right_transfer[0])
-    low = sent(raw, [(r, r + 1) for r in range(0, row_count, 2)])
-    own, two, block = operators(ranks, initial, raw, low)
+    swap = [(r, r + 1) for r in range(0, row_count, 2)]
+    right_low = sent(right_transfer[0], swap)
+    left_low = sent(left_transfer[0, 0], swap)
+    padded = jnp.pad(left_transfer[0, 0], ((0, 0), (0, boundary_in.shape[2] - block_size)))
+    stacked = jnp.concatenate([boundary_in[0], right_transfer[0], padded], axis=0)
+    own, two, initial, block = operators(ranks, stacked, left_low, right_low)
     arrived = sent(block, [(1, 3)])
     half = sent(two, [(r, r + 2) for r in range(5, row_count, 4)])
 
+    last = row_count - 5
     source = jnp.where(row == 3, arrived, initial)
-    block = taken(two, arrived)
+    (block,) = taken(two, arrived)
     leaving = block
     four = joined(two, half)
-    hops = list(range(3, row_count - 4, 4))
-    for last in hops:
-        arrived = sent(block, [(last, last + 4)])
-        source = jnp.where(row == last + 4, arrived, source)
-        if last != hops[-1]:
-            block = taken(four, arrived)
-            leaving = jnp.where(row == last + 4, block, leaving)
-
-    arrived = sent(leaving, [(r, r + 2) for r in range(3, row_count - 2, 4)])
-    to_first = [(r + 1, r) for r in range(2, row_count, 2)]
-    relayed = sent(half, to_first[2::2])
-    source = jnp.where((row % 4 == 1) & (row > 1), arrived, source)
-    arrived = sent(source, to_first)
+    hops = list(range(3, last, 4))
+    for hop, start in enumerate(hops):
+        arrived = sent(block, [(start, start + 4)])
+        source = jnp.where(row == start + 4, arrived, source)
+        end = hop == len(hops) - 1
+        if end:
+            spread = sent(leaving, [(r, r + 2) for r in hops])
+            relayed = sent(half, [(r + 1, r) for r in range(6, row_count, 4)])
+        block, *more = taken(four, arrived, copies=2 if end else 1)
+        if not end:
+            leaving = jnp.where(row == start + 4, block, leaving)
+    for_end = sent(block, [(last, last + 3)])
+    for_spread = sent(more[0], [(last, last + 1)])
+    source = jnp.where((row % 4 == 1) & (row > 1), spread, source)
+    arrived = sent(source, [(r + 1, r) for r in range(2, last, 2)])
     source = jnp.where((row % 2 == 0) & (row > 0), arrived, source)
+    source = jnp.where(row == last + 3, for_end, source)
+    source = jnp.where(row == last + 1, for_spread, source)
+    arrived = sent(source, [(last + 1, last + 2), (last + 3, last + 4)])
+    source = jnp.where((row == last + 2) | (row == last + 4), arrived, source)
     second = row % 2 == 1
     base = jnp.where(second, two, own)
     final = joined(base, jnp.where(second, half, relayed))

time: 68.3 us -> 67.2 us (0.984)
  the two profiles are of different devices: /device:TPU:384 before, /device:TPU:448 now
where the time goes in v2:
time: 67.2 us; the launch traced here: 66.8 us
  waiting for transfers between devices  23.9 us (36%)
  starting transfers between devices  17.1 us (25%)
  blocking collectives  15.9 us (24%)
  Pallas kernels  5.59 us (8%)
  other arithmetic  2.46 us (4%)
  between operations  1.66 us (2%)
    all_to_all x1, blocking collectives, on_device(): lax.all_to_all(sums, 'sector', 0, 0, axis_index_groups=lines, tiled=True)  15.9 us
    ppermute x12, waiting for transfers between devices, sent(): return lax.ppermute(value, 'row', pairs)  13.1 us
    ppermute x12, starting transfers between devices, sent(): return lax.ppermute(value, 'row', pairs)  11.8 us
    all_to_all x1, waiting for transfers between devices, on_device(): lax.all_to_all(outgoing, 'sector', 0, 0, axis_index_groups=tiles, tiled=T...  10.9 us
    all_to_all x1, starting transfers between devices, on_device(): lax.all_to_all(outgoing, 'sector', 0, 0, axis_index_groups=tiles, tiled=T...  5.31 us
    pallas_call x7, Pallas kernels, on_core(): pl.pallas_call(kernel, out_shape=shapes, in_specs=[whole(space) for space...  3.73 us
    pallas_call x1, Pallas kernels, environment_sums(): pl.pallas_call(kernel, out_shape=jax.ShapeDtypeStruct((targets, rows, col...  1.86 us
  transfers between devices with their start and end apart: 13, of which 3 were waited for; matrix products, arithmetic and copies ran while one was open for 2% of the time, Pallas kernels for 2%

profile of v2, /device:TPU:448, one launch (start us, length us, event | category | flops | bytes accessed | tf_op | source)
XLA Modules:
  0.0 66.8 jit_solution(3421272742451959907)
XLA Ops:
  0.6 0.0 copy-start.1
  0.6 0.0 copy-start.2
  0.7 1.9 %collective-permute-start.1 = (f32[256,256]{1,0:T(8,128)}, f32[256,256]{1,0:T(8,128)S(1)}, u32[]{:S(2)}, u32[]{:S(2)}) collective-permute-start(f32[256,256]{1,0:T(8,128)} %bitcast.11), channel_id=1, source_target_pairs={{0,32},{64,96},{128,160},{192,224},{256,288},{320,352},{384,416},{... | collective-permute-start | bytes 786440 | tf_op jit(solution)/shard_map/ppermute | solution.py:176
  2.5 1.3 %collective-permute-start = (f32[128,128]{1,0:T(8,128)}, f32[128,128]{1,0:T(8,128)S(1)}, u32[]{:S(2)}, u32[]{:S(2)}) collective-permute-start(f32[128,128]{1,0:T(8,128)} %bitcast.15), channel_id=1, source_target_pairs={{0,32},{64,96},{128,160},{192,224},{256,288},{320,352},{384,416},{... | collective-permute-start | bytes 196616 | tf_op jit(solution)/shard_map/ppermute | solution.py:176
  4.5 1.1 %select_maximum_fusion.stacked_ref = f32[512,256]{1,0:T(8,128)S(1)} fusion(f32[128,128]{1,0:T(8,128)} %bitcast.16, f32[256,256]{1,0:T(8,128)} %bitcast.12, f32[128,256]{1,0:T(8,128)} %bitcast.13), kind=kLoop, calls=%fused_computation | loop fusion | flops 524288 | bytes 983040 | tf_op jit(solution)/shard_map/concatenate | solution.py:182
  5.6 0.0 collective-permute-done.left_low_ref
  5.6 0.0 collective-permute-done.1.right_low_ref
  5.6 0.6 shard_map.86
  6.2 0.7 %collective-permute-start.2 = (f32[320,256]{1,0:T(8,128)S(1)}, f32[320,256]{1,0:T(8,128)S(1)}, u32[]{:S(2)}, u32[]{:S(2)}) collective-permute-start(f32[320,256]{1,0:T(8,128)S(1)} %get-tuple-element.10.later_ref.operator_ref), channel_id=1, source_target_pairs={{160,224},{288,352},{416,480},{161,225},{289,353},{417,481},{162,2... | collective-permute-start | bytes 983048 | tf_op jit(solution)/shard_map/ppermute | solution.py:176
  6.9 0.7 %collective-permute-start.4 = (f32[128,256]{1,0:T(8,128)S(1)}, f32[128,256]{1,0:T(8,128)S(1)}, u32[]{:S(2)}, u32[]{:S(2)}) collective-permute-start(f32[128,256]{1,0:T(8,128)S(1)} %get-tuple-element.12), channel_id=1, source_target_pairs={{32,96},{33,97},{34,98},{35,99},{36,100},{37,101},{38,102},{39,103... | collective-permute-start | bytes 393224 | tf_op jit(solution)/shard_map/ppermute | solution.py:176
  7.6 0.0 collective-permute-done.4.block_ref
  7.6 0.4 shard_map.89
  8.0 0.7 %collective-permute-start.5 = (f32[128,256]{1,0:T(8,128)S(1)}, f32[128,256]{1,0:T(8,128)S(1)}, u32[]{:S(2)}, u32[]{:S(2)}) collective-permute-start(f32[128,256]{1,0:T(8,128)S(1)} %shard_map.89), channel_id=1, source_target_pairs={{96,224},{97,225},{98,226},{99,227},{100,228},{101,229},{102,230},... | collective-permute-start | bytes 393224 | tf_op jit(solution)/shard_map/ppermute | solution.py:176
  8.7 0.0 copy-done.1
  8.7 0.0 copy-done.2
  8.7 0.2 select_reduce_fusion.1
  8.9 0.0 collective-permute-done.2.earlier_ref
  8.9 0.3 shard_map.88.operator_ref
  9.2 0.0 collective-permute-done.5.block_ref
  9.2 0.4 shard_map.90
  9.6 0.7 %collective-permute-start.6 = (f32[128,256]{1,0:T(8,128)S(1)}, f32[128,256]{1,0:T(8,128)S(1)}, u32[]{:S(2)}, u32[]{:S(2)}) collective-permute-start(f32[128,256]{1,0:T(8,128)S(1)} %shard_map.90), channel_id=1, source_target_pairs={{224,352},{225,353},{226,354},{227,355},{228,356},{229,357},{230,3... | collective-permute-start | bytes 393224 | tf_op jit(solution)/shard_map/ppermute | solution.py:176
  10.3 0.7 %collective-permute-start.9 = (f32[128,256]{1,0:T(8,128)S(1)}, f32[128,256]{1,0:T(8,128)S(1)}, u32[]{:S(2)}, u32[]{:S(2)}) collective-permute-start(f32[128,256]{1,0:T(8,128)S(1)} %broadcast_select_fusion.3), channel_id=1, source_target_pairs={{96,160},{224,288},{97,161},{225,289},{98,162},{226,290},{99,163},... | collective-permute-start | bytes 393224 | tf_op jit(solution)/shard_map/ppermute | solution.py:176
  11.1 0.1 select_reduce_fusion
  11.2 1.3 %collective-permute-start.3 = (f32[320,256]{1,0:T(8,128)S(1)}, f32[320,256]{1,0:T(8,128)S(1)}, u32[]{:S(2)}, u32[]{:S(2)}) collective-permute-start(f32[320,256]{1,0:T(8,128)S(1)} %collective-permute-done.2.earlier_ref), channel_id=1, source_target_pairs={{224,192},{352,320},{480,448},{225,193},{353,321},{481,449},{226,1... | collective-permute-start | bytes 983048 | tf_op jit(solution)/shard_map/ppermute | solution.py:176
  12.5 0.0 collective-permute-done.6.block_ref
  12.5 0.4 shard_map.91
  12.9 0.7 %collective-permute-start.7 = (f32[128,256]{1,0:T(8,128)S(1)}, f32[128,256]{1,0:T(8,128)S(1)}, u32[]{:S(2)}, u32[]{:S(2)}) collective-permute-start(f32[128,256]{1,0:T(8,128)S(1)} %get-tuple-element.13), channel_id=1, source_target_pairs={{352,384},{353,385},{354,386},{355,387},{356,388},{357,389},{358,3... | collective-permute-start | bytes 393224 | tf_op jit(solution)/shard_map/ppermute | solution.py:176
  13.6 1.3 %collective-permute-start.8 = (f32[128,256]{1,0:T(8,128)S(1)}, f32[128,256]{1,0:T(8,128)S(1)}, u32[]{:S(2)}, u32[]{:S(2)}) collective-permute-start(f32[128,256]{1,0:T(8,128)S(1)} %get-tuple-element.14), channel_id=1, source_target_pairs={{352,448},{353,449},{354,450},{355,451},{356,452},{357,453},{358,4... | collective-permute-start | bytes 393224 | tf_op jit(solution)/shard_map/ppermute | solution.py:176
  14.9 0.0 collective-permute-done.9
  14.9 0.7 %collective-permute-start.10 = (f32[128,256]{1,0:T(8,128)S(1)}, f32[128,256]{1,0:T(8,128)S(1)}, u32[]{:S(2)}, u32[]{:S(2)}) collective-permute-start(f32[128,256]{1,0:T(8,128)S(1)} %select_select_fusion.1), channel_id=1, source_target_pairs={{96,64},{160,128},{224,192},{288,256},{352,320},{97,65},{161,129},... | collective-permute-start | bytes 393224 | tf_op jit(solution)/shard_map/ppermute | solution.py:176
  15.7 0.0 collective-permute-done.7
  15.7 12.5 %collective-permute-done.8 = f32[128,256]{1,0:T(8,128)S(1)} collective-permute-done((f32[128,256]{1,0:T(8,128)S(1)}, f32[128,256]{1,0:T(8,128)S(1)}, u32[]{:S(2)}, u32[]{:S(2)}) %collective-permute-start.8) | collective-permute-done | bytes 131104 | tf_op jit(solution)/shard_map/ppermute | solution.py:176
  28.2 0.0 collective-permute-done.10
  28.2 1.3 %collective-permute-start.11 = (f32[128,256]{1,0:T(8,128)S(1)}, f32[128,256]{1,0:T(8,128)S(1)}, u32[]{:S(2)}, u32[]{:S(2)}) collective-permute-start(f32[128,256]{1,0:T(8,128)S(1)} %select_select_fusion), channel_id=1, source_target_pairs={{384,416},{448,480},{385,417},{449,481},{386,418},{450,482},{387,4... | collective-permute-start | bytes 393224 | tf_op jit(solution)/shard_map/ppermute | solution.py:176
  29.5 0.0 collective-permute-done.3
  29.6 0.0 copy-start
  29.6 0.3 shard_map.87
  30.0 0.5 collective-permute-done.11
  30.5 1.3 %shard_map.92 = (f32[128,256]{1,0:T(8,128)}, bf16[8,136,256]{2,1,0:T(8,128)(2,1)}) custom-call(f32[320,256]{1,0:T(8,128)S(1)} %broadcast_select_fusion.2.operator_ref, f32[128,256]{1,0:T(8,128)S(1)} %broadcast_select_fusion.4.block_ref, bf16[8,256]{1,0:T(8,128)(2,1)S(1)} %broadcast_in_dim.6.extra_ref), custom_call_target="tpu_custom_call" | custom-call | flops 119537664 | bytes 933888 | tf_op jit(solution)/shard_map/pallas_call | solution.py:54
  31.8 5.3 %all-to-all-start = ((bf16[8,136,256]{2,1,0:T(8,128)(2,1)}), bf16[8,136,256]{2,1,0:T(8,128)(2,1)S(1)}, u32[]{:S(2)}, u32[]{:S(2)}) async-start(bf16[8,136,256]{2,1,0:T(8,128)(2,1)} %get-tuple-element.17), calls=%async_computation | async-start | bytes 1114112 | tf_op jit(solution)/shard_map/all_to_all | solution.py:236
  37.1 0.1 fusion
  37.2 10.9 %all-to-all-done.arrived_ref = bf16[8,136,256]{2,1,0:T(8,128)(2,1)S(1)} async-done(((bf16[8,136,256]{2,1,0:T(8,128)(2,1)}), bf16[8,136,256]{2,1,0:T(8,128)(2,1)S(1)}, u32[]{:S(2)}, u32[]{:S(2)}) %all-to-all-start) | async-done | bytes 557088 | tf_op jit(solution)/shard_map/all_to_all | solution.py:236
  48.1 0.1 multiply_reduce_fusion
  48.2 0.1 copy.9
  48.3 0.0 copy-done
  48.3 1.9 %shard_map.93 = bf16[4,128,256]{2,1,0:T(8,128)(2,1)S(1)} custom-call(s32[8,4]{1,0:T(8,128)S(1)} %convert_add_fusion.slots_ref, bf16[8,136,256]{2,1,0:T(8,128)(2,1)S(1)} %all-to-all-done.arrived_ref, bf16[16,256,256]{2,1,0:T(8,128)(2,1)S(1)} %bitcast.10), custom_call_target="tpu_custom_call" | custom-call | flops 536870912 | bytes 2916352 | tf_op jit(solution)/shard_map/pallas_call | solution.py:154
  50.1 15.9 %all_to_all.10 = bf16[4,128,256]{2,1,0:T(8,128)(2,1)S(1)} all-to-all(bf16[4,128,256]{2,1,0:T(8,128)(2,1)S(1)} %shard_map.93), channel_id=1, replica_groups={{0,2,4,6},{1,3,5,7},{8,10,12,14},{9,11,13,15},{16,18,20,22},{17,19,21,2..., dimensions={0} | all-to-all | bytes 524288 | tf_op jit(solution)/shard_map/all_to_all | solution.py:244
  66.1 0.7 %convert_reduce_fusion = f32[128,256]{1,0:T(8,128)} fusion(bf16[4,128,256]{2,1,0:T(8,128)(2,1)S(1)} %all_to_all.10), kind=kLoop, calls=%fused_computation.2 | loop fusion | flops 229376 | bytes 393216 | tf_op jit(solution)/shard_map/reduce_sum | solution.py:245
  (14 shorter events, 0.3 us)
Async XLA Ops:
  0.6 8.0 %copy-start.1 = (s32[32]{0:T(128)S(1)}, s32[32]{0:T(128)}, u32[]{:S(2)}) copy-start(s32[32]{0:T(128)} %param.13) | copy-start | bytes 388
  0.6 8.0 %copy-start.2 = (s32[1,16]{1,0:T(1,128)S(1)}, s32[1,16]{1,0:T(1,128)}, u32[]{:S(2)}) copy-start(s32[1,16]{1,0:T(1,128)} %param.12) | copy-start | bytes 196
  0.7 4.9 %collective-permute-start.1 = (f32[256,256]{1,0:T(8,128)}, f32[256,256]{1,0:T(8,128)S(1)}, u32[]{:S(2)}, u32[]{:S(2)}) collective-permute-start(f32[256,256]{1,0:T(8,128)} %bitcast.11), channel_id=1, source_target_pairs={{0,32},{64,96},{128,160},{192,224},{256,288},{320,352},{384,416},{... | collective-permute-start | bytes 786440 | tf_op jit(solution)/shard_map/ppermute | solution.py:176
  2.5 3.0 %collective-permute-start = (f32[128,128]{1,0:T(8,128)}, f32[128,128]{1,0:T(8,128)S(1)}, u32[]{:S(2)}, u32[]{:S(2)}) collective-permute-start(f32[128,128]{1,0:T(8,128)} %bitcast.15), channel_id=1, source_target_pairs={{0,32},{64,96},{128,160},{192,224},{256,288},{320,352},{384,416},{... | collective-permute-start | bytes 196616 | tf_op jit(solution)/shard_map/ppermute | solution.py:176
  6.2 2.7 %collective-permute-start.2 = (f32[320,256]{1,0:T(8,128)S(1)}, f32[320,256]{1,0:T(8,128)S(1)}, u32[]{:S(2)}, u32[]{:S(2)}) collective-permute-start(f32[320,256]{1,0:T(8,128)S(1)} %get-tuple-element.10.later_ref.operator_ref), channel_id=1, source_target_pairs={{160,224},{288,352},{416,480},{161,225},{289,353},{417,481},{162,2... | collective-permute-start | bytes 983048 | tf_op jit(solution)/shard_map/ppermute | solution.py:176
  6.9 0.7 %collective-permute-start.4 = (f32[128,256]{1,0:T(8,128)S(1)}, f32[128,256]{1,0:T(8,128)S(1)}, u32[]{:S(2)}, u32[]{:S(2)}) collective-permute-start(f32[128,256]{1,0:T(8,128)S(1)} %get-tuple-element.12), channel_id=1, source_target_pairs={{32,96},{33,97},{34,98},{35,99},{36,100},{37,101},{38,102},{39,103... | collective-permute-start | bytes 393224 | tf_op jit(solution)/shard_map/ppermute | solution.py:176
  8.0 1.2 %collective-permute-start.5 = (f32[128,256]{1,0:T(8,128)S(1)}, f32[128,256]{1,0:T(8,128)S(1)}, u32[]{:S(2)}, u32[]{:S(2)}) collective-permute-start(f32[128,256]{1,0:T(8,128)S(1)} %shard_map.89), channel_id=1, source_target_pairs={{96,224},{97,225},{98,226},{99,227},{100,228},{101,229},{102,230},... | collective-permute-start | bytes 393224 | tf_op jit(solution)/shard_map/ppermute | solution.py:176
  9.6 2.8 %collective-permute-start.6 = (f32[128,256]{1,0:T(8,128)S(1)}, f32[128,256]{1,0:T(8,128)S(1)}, u32[]{:S(2)}, u32[]{:S(2)}) collective-permute-start(f32[128,256]{1,0:T(8,128)S(1)} %shard_map.90), channel_id=1, source_target_pairs={{224,352},{225,353},{226,354},{227,355},{228,356},{229,357},{230,3... | collective-permute-start | bytes 393224 | tf_op jit(solution)/shard_map/ppermute | solution.py:176
  10.3 4.5 %collective-permute-start.9 = (f32[128,256]{1,0:T(8,128)S(1)}, f32[128,256]{1,0:T(8,128)S(1)}, u32[]{:S(2)}, u32[]{:S(2)}) collective-permute-start(f32[128,256]{1,0:T(8,128)S(1)} %broadcast_select_fusion.3), channel_id=1, source_target_pairs={{96,160},{224,288},{97,161},{225,289},{98,162},{226,290},{99,163},... | collective-permute-start | bytes 393224 | tf_op jit(solution)/shard_map/ppermute | solution.py:176
  11.2 18.4 %collective-permute-start.3 = (f32[320,256]{1,0:T(8,128)S(1)}, f32[320,256]{1,0:T(8,128)S(1)}, u32[]{:S(2)}, u32[]{:S(2)}) collective-permute-start(f32[320,256]{1,0:T(8,128)S(1)} %collective-permute-done.2.earlier_ref), channel_id=1, source_target_pairs={{224,192},{352,320},{480,448},{225,193},{353,321},{481,449},{226,1... | collective-permute-start | bytes 983048 | tf_op jit(solution)/shard_map/ppermute | solution.py:176
  12.9 2.8 %collective-permute-start.7 = (f32[128,256]{1,0:T(8,128)S(1)}, f32[128,256]{1,0:T(8,128)S(1)}, u32[]{:S(2)}, u32[]{:S(2)}) collective-permute-start(f32[128,256]{1,0:T(8,128)S(1)} %get-tuple-element.13), channel_id=1, source_target_pairs={{352,384},{353,385},{354,386},{355,387},{356,388},{357,389},{358,3... | collective-permute-start | bytes 393224 | tf_op jit(solution)/shard_map/ppermute | solution.py:176
  13.6 14.6 %collective-permute-start.8 = (f32[128,256]{1,0:T(8,128)S(1)}, f32[128,256]{1,0:T(8,128)S(1)}, u32[]{:S(2)}, u32[]{:S(2)}) collective-permute-start(f32[128,256]{1,0:T(8,128)S(1)} %get-tuple-element.14), channel_id=1, source_target_pairs={{352,448},{353,449},{354,450},{355,451},{356,452},{357,453},{358,4... | collective-permute-start | bytes 393224 | tf_op jit(solution)/shard_map/ppermute | solution.py:176
  14.9 13.3 %collective-permute-start.10 = (f32[128,256]{1,0:T(8,128)S(1)}, f32[128,256]{1,0:T(8,128)S(1)}, u32[]{:S(2)}, u32[]{:S(2)}) collective-permute-start(f32[128,256]{1,0:T(8,128)S(1)} %select_select_fusion.1), channel_id=1, source_target_pairs={{96,64},{160,128},{224,192},{288,256},{352,320},{97,65},{161,129},... | collective-permute-start | bytes 393224 | tf_op jit(solution)/shard_map/ppermute | solution.py:176
  28.2 2.3 %collective-permute-start.11 = (f32[128,256]{1,0:T(8,128)S(1)}, f32[128,256]{1,0:T(8,128)S(1)}, u32[]{:S(2)}, u32[]{:S(2)}) collective-permute-start(f32[128,256]{1,0:T(8,128)S(1)} %select_select_fusion), channel_id=1, source_target_pairs={{384,416},{448,480},{385,417},{449,481},{386,418},{450,482},{387,4... | collective-permute-start | bytes 393224 | tf_op jit(solution)/shard_map/ppermute | solution.py:176
  29.6 18.7 %copy-start = (bf16[1,16,256,256]{3,2,1,0:T(8,128)(2,1)S(1)}, bf16[1,16,256,256]{3,2,1,0:T(8,128)(2,1)}, u32[]{:S(2)}) copy-start(bf16[1,16,256,256]{3,2,1,0:T(8,128)(2,1)} %param.10) | copy-start | bytes 6291460
  31.8 16.3 %all-to-all-start = ((bf16[8,136,256]{2,1,0:T(8,128)(2,1)}), bf16[8,136,256]{2,1,0:T(8,128)(2,1)S(1)}, u32[]{:S(2)}, u32[]{:S(2)}) async-start(bf16[8,136,256]{2,1,0:T(8,128)(2,1)} %get-tuple-element.17), calls=%async_computation | async-start | bytes 1114112 | tf_op jit(solution)/shard_map/all_to_all | solution.py:236

commit v3 on v2

--- a/solution.py
+++ b/solution.py
@@ -8,6 +8,8 @@
 ALONG = 8
 PAIR = 2
 EXTRA = 8
+TILE_ORDER = (2, 3, 0, 1)
+LINE_ORDER = (2, 3, 0, 1)
 VMEM_GRANT = 8 * 1024 * 1024
 
 
@@ -149,7 +151,8 @@
             sums_ref[target] = total.astype(jnp.bfloat16)
             return carried
 
-        lax.fori_loop(0, targets, one_target, 0)
+        for target in range(targets):
+            one_target(target, 0)
 
     return pl.pallas_call(
         kernel,
@@ -218,11 +221,11 @@
     across = sector_count // along
     parts = along // PAIR
     tiles = [
-        [x * along + part * PAIR + y for x in range(across) for y in range(PAIR)]
+        [x * along + part * PAIR + y for x in TILE_ORDER for y in range(PAIR)]
         for part in range(parts)
     ]
     lines = [
-        [x * along + part * PAIR + y for part in range(parts)]
+        [x * along + part * PAIR + y for part in LINE_ORDER]
         for x in range(across)
         for y in range(PAIR)
     ]
@@ -237,7 +240,7 @@
         outgoing,
         "sector", 0, 0, axis_index_groups=tiles, tiled=True,
     )
-    targets = (sector // along) * along + sector % PAIR + jnp.arange(parts) * PAIR
+    targets = (sector // along) * along + sector % PAIR + jnp.asarray(LINE_ORDER) * PAIR
     wanted = (jnp.arange(block_size * 2)[None, :] == targets[:, None]).astype(jnp.float32)
     slots = jnp.sum(arrived[:, block_size, None, :].astype(jnp.float32) * wanted[None], axis=2)
     sums = environment_sums(slots.astype(jnp.int32) - 1, arrived, env_weight[0])

time: 67.2 us -> 64.2 us (0.955)
  the two profiles are of different devices: /device:TPU:448 before, /device:TPU:449 now
where the time goes in v3:
time: 64.2 us; the launch traced here: 63.8 us
  waiting for transfers between devices  22 us (34%)
  starting transfers between devices  17.5 us (27%)
  blocking collectives  15.1 us (24%)
  Pallas kernels  5.04 us (8%)
  other arithmetic  2.46 us (4%)
  between operations  1.67 us (3%)
    all_to_all x1, blocking collectives, on_device(): lax.all_to_all(sums, 'sector', 0, 0, axis_index_groups=lines, tiled=True)  15.1 us
    ppermute x12, waiting for transfers between devices, sent(): return lax.ppermute(value, 'row', pairs)  14 us
    ppermute x12, starting transfers between devices, sent(): return lax.ppermute(value, 'row', pairs)  11.3 us
    all_to_all x1, waiting for transfers between devices, on_device(): lax.all_to_all(outgoing, 'sector', 0, 0, axis_index_groups=tiles, tiled=T...  7.92 us
    all_to_all x1, starting transfers between devices, on_device(): lax.all_to_all(outgoing, 'sector', 0, 0, axis_index_groups=tiles, tiled=T...  6.2 us
    pallas_call x7, Pallas kernels, on_core(): pl.pallas_call(kernel, out_shape=shapes, in_specs=[whole(space) for space...  3.72 us
    pallas_call x1, Pallas kernels, environment_sums(): pl.pallas_call(kernel, out_shape=jax.ShapeDtypeStruct((targets, rows, col...  1.32 us
  transfers between devices with their start and end apart: 13, of which 4 were waited for; matrix products, arithmetic and copies ran while one was open for 3% of the time, Pallas kernels for 2%

profile of v3, /device:TPU:449, one launch (start us, length us, event | category | flops | bytes accessed | tf_op | source)
XLA Modules:
  0.0 63.8 jit_solution(7764216855377768652)
XLA Ops:
  0.6 0.0 copy-start.1
  0.6 0.0 copy-start.2
  0.7 1.4 %collective-permute-start.1 = (f32[256,256]{1,0:T(8,128)}, f32[256,256]{1,0:T(8,128)S(1)}, u32[]{:S(2)}, u32[]{:S(2)}) collective-permute-start(f32[256,256]{1,0:T(8,128)} %bitcast.11), channel_id=1, source_target_pairs={{0,32},{64,96},{128,160},{192,224},{256,288},{320,352},{384,416},{... | collective-permute-start | bytes 786440 | tf_op jit(solution)/shard_map/ppermute | solution.py:179
  2.1 1.3 %collective-permute-start = (f32[128,128]{1,0:T(8,128)}, f32[128,128]{1,0:T(8,128)S(1)}, u32[]{:S(2)}, u32[]{:S(2)}) collective-permute-start(f32[128,128]{1,0:T(8,128)} %bitcast.15), channel_id=1, source_target_pairs={{0,32},{64,96},{128,160},{192,224},{256,288},{320,352},{384,416},{... | collective-permute-start | bytes 196616 | tf_op jit(solution)/shard_map/ppermute | solution.py:179
  4.0 1.1 %select_maximum_fusion.stacked_ref = f32[512,256]{1,0:T(8,128)S(1)} fusion(f32[128,128]{1,0:T(8,128)} %bitcast.16, f32[256,256]{1,0:T(8,128)} %bitcast.12, f32[128,256]{1,0:T(8,128)} %bitcast.13), kind=kLoop, calls=%fused_computation | loop fusion | flops 524288 | bytes 983040 | tf_op jit(solution)/shard_map/concatenate | solution.py:185
  5.1 0.4 collective-permute-done.left_low_ref
  5.5 0.0 collective-permute-done.1.right_low_ref
  5.5 0.6 shard_map.95
  6.1 1.3 %collective-permute-start.2 = (f32[320,256]{1,0:T(8,128)S(1)}, f32[320,256]{1,0:T(8,128)S(1)}, u32[]{:S(2)}, u32[]{:S(2)}) collective-permute-start(f32[320,256]{1,0:T(8,128)S(1)} %get-tuple-element.10.later_ref.operator_ref), channel_id=1, source_target_pairs={{160,224},{288,352},{416,480},{161,225},{289,353},{417,481},{162,2... | collective-permute-start | bytes 983048 | tf_op jit(solution)/shard_map/ppermute | solution.py:179
  7.4 0.7 %collective-permute-start.4 = (f32[128,256]{1,0:T(8,128)S(1)}, f32[128,256]{1,0:T(8,128)S(1)}, u32[]{:S(2)}, u32[]{:S(2)}) collective-permute-start(f32[128,256]{1,0:T(8,128)S(1)} %get-tuple-element.12), channel_id=1, source_target_pairs={{32,96},{33,97},{34,98},{35,99},{36,100},{37,101},{38,102},{39,103... | collective-permute-start | bytes 393224 | tf_op jit(solution)/shard_map/ppermute | solution.py:179
  8.1 0.0 collective-permute-done.4.block_ref
  8.1 0.4 shard_map.98
  8.5 0.7 %collective-permute-start.5 = (f32[128,256]{1,0:T(8,128)S(1)}, f32[128,256]{1,0:T(8,128)S(1)}, u32[]{:S(2)}, u32[]{:S(2)}) collective-permute-start(f32[128,256]{1,0:T(8,128)S(1)} %shard_map.98), channel_id=1, source_target_pairs={{96,224},{97,225},{98,226},{99,227},{100,228},{101,229},{102,230},... | collective-permute-start | bytes 393224 | tf_op jit(solution)/shard_map/ppermute | solution.py:179
  9.2 0.0 copy-done.1
  9.2 0.0 copy-done.2
  9.2 0.2 select_reduce_fusion.1
  9.4 4.5 %collective-permute-done.2.earlier_ref = f32[320,256]{1,0:T(8,128)S(1)} collective-permute-done((f32[320,256]{1,0:T(8,128)S(1)}, f32[320,256]{1,0:T(8,128)S(1)}, u32[]{:S(2)}, u32[]{:S(2)}) %collective-permute-start.2) | collective-permute-done | bytes 327712 | tf_op jit(solution)/shard_map/ppermute | solution.py:179
  13.9 0.3 shard_map.97.operator_ref
  14.2 0.0 collective-permute-done.5.block_ref
  14.2 0.4 shard_map.99
  14.6 0.7 %collective-permute-start.6 = (f32[128,256]{1,0:T(8,128)S(1)}, f32[128,256]{1,0:T(8,128)S(1)}, u32[]{:S(2)}, u32[]{:S(2)}) collective-permute-start(f32[128,256]{1,0:T(8,128)S(1)} %shard_map.99), channel_id=1, source_target_pairs={{224,352},{225,353},{226,354},{227,355},{228,356},{229,357},{230,3... | collective-permute-start | bytes 393224 | tf_op jit(solution)/shard_map/ppermute | solution.py:179
  15.3 0.7 %collective-permute-start.9 = (f32[128,256]{1,0:T(8,128)S(1)}, f32[128,256]{1,0:T(8,128)S(1)}, u32[]{:S(2)}, u32[]{:S(2)}) collective-permute-start(f32[128,256]{1,0:T(8,128)S(1)} %broadcast_select_fusion.3), channel_id=1, source_target_pairs={{96,160},{224,288},{97,161},{225,289},{98,162},{226,290},{99,163},... | collective-permute-start | bytes 393224 | tf_op jit(solution)/shard_map/ppermute | solution.py:179
  16.1 0.1 select_reduce_fusion
  16.2 1.3 %collective-permute-start.3 = (f32[320,256]{1,0:T(8,128)S(1)}, f32[320,256]{1,0:T(8,128)S(1)}, u32[]{:S(2)}, u32[]{:S(2)}) collective-permute-start(f32[320,256]{1,0:T(8,128)S(1)} %collective-permute-done.2.earlier_ref), channel_id=1, source_target_pairs={{224,192},{352,320},{480,448},{225,193},{353,321},{481,449},{226,1... | collective-permute-start | bytes 983048 | tf_op jit(solution)/shard_map/ppermute | solution.py:179
  17.5 0.0 collective-permute-done.6.block_ref
  17.5 0.4 shard_map.100
  17.9 0.7 %collective-permute-start.7 = (f32[128,256]{1,0:T(8,128)S(1)}, f32[128,256]{1,0:T(8,128)S(1)}, u32[]{:S(2)}, u32[]{:S(2)}) collective-permute-start(f32[128,256]{1,0:T(8,128)S(1)} %get-tuple-element.13), channel_id=1, source_target_pairs={{352,384},{353,385},{354,386},{355,387},{356,388},{357,389},{358,3... | collective-permute-start | bytes 393224 | tf_op jit(solution)/shard_map/ppermute | solution.py:179
  18.6 0.7 %collective-permute-start.8 = (f32[128,256]{1,0:T(8,128)S(1)}, f32[128,256]{1,0:T(8,128)S(1)}, u32[]{:S(2)}, u32[]{:S(2)}) collective-permute-start(f32[128,256]{1,0:T(8,128)S(1)} %get-tuple-element.14), channel_id=1, source_target_pairs={{352,448},{353,449},{354,450},{355,451},{356,452},{357,453},{358,4... | collective-permute-start | bytes 393224 | tf_op jit(solution)/shard_map/ppermute | solution.py:179
  19.3 0.0 collective-permute-done.9
  19.3 0.7 %collective-permute-start.10 = (f32[128,256]{1,0:T(8,128)S(1)}, f32[128,256]{1,0:T(8,128)S(1)}, u32[]{:S(2)}, u32[]{:S(2)}) collective-permute-start(f32[128,256]{1,0:T(8,128)S(1)} %select_select_fusion.1), channel_id=1, source_target_pairs={{96,64},{160,128},{224,192},{288,256},{352,320},{97,65},{161,129},... | collective-permute-start | bytes 393224 | tf_op jit(solution)/shard_map/ppermute | solution.py:179
  20.1 0.0 collective-permute-done.7
  20.1 0.0 collective-permute-done.8
  20.1 0.0 collective-permute-done.10
  20.1 1.3 %collective-permute-start.11 = (f32[128,256]{1,0:T(8,128)S(1)}, f32[128,256]{1,0:T(8,128)S(1)}, u32[]{:S(2)}, u32[]{:S(2)}) collective-permute-start(f32[128,256]{1,0:T(8,128)S(1)} %select_select_fusion), channel_id=1, source_target_pairs={{384,416},{448,480},{385,417},{449,481},{386,418},{450,482},{387,4... | collective-permute-start | bytes 393224 | tf_op jit(solution)/shard_map/ppermute | solution.py:179
  21.4 0.0 collective-permute-done.3
  21.5 0.0 copy-start.3
  21.5 0.0 copy-start
  21.5 0.3 shard_map.96
  21.9 9.1 %collective-permute-done.11 = f32[128,256]{1,0:T(8,128)S(1)} collective-permute-done((f32[128,256]{1,0:T(8,128)S(1)}, f32[128,256]{1,0:T(8,128)S(1)}, u32[]{:S(2)}, u32[]{:S(2)}) %collective-permute-start.11) | collective-permute-done | bytes 131104 | tf_op jit(solution)/shard_map/ppermute | solution.py:179
  31.1 1.3 %shard_map.101 = (f32[128,256]{1,0:T(8,128)}, bf16[8,136,256]{2,1,0:T(8,128)(2,1)}) custom-call(f32[320,256]{1,0:T(8,128)S(1)} %broadcast_select_fusion.2.operator_ref, f32[128,256]{1,0:T(8,128)S(1)} %broadcast_select_fusion.4.block_ref, bf16[8,256]{1,0:T(8,128)(2,1)S(1)} %broadcast_in_dim.6.extra_ref), custom_call_target="tpu_custom_call" | custom-call | flops 119537664 | bytes 933888 | tf_op jit(solution)/shard_map/pallas_call | solution.py:56
  32.3 6.2 %all-to-all-start = ((bf16[8,136,256]{2,1,0:T(8,128)(2,1)}), bf16[8,136,256]{2,1,0:T(8,128)(2,1)S(1)}, u32[]{:S(2)}, u32[]{:S(2)}) async-start(bf16[8,136,256]{2,1,0:T(8,128)(2,1)} %get-tuple-element.17), calls=%async_computation | async-start | bytes 1114112 | tf_op jit(solution)/shard_map/all_to_all | solution.py:239
  38.5 0.1 fusion
  38.6 7.9 %all-to-all-done.arrived_ref = bf16[8,136,256]{2,1,0:T(8,128)(2,1)S(1)} async-done(((bf16[8,136,256]{2,1,0:T(8,128)(2,1)}), bf16[8,136,256]{2,1,0:T(8,128)(2,1)S(1)}, u32[]{:S(2)}, u32[]{:S(2)}) %all-to-all-start) | async-done | bytes 557088 | tf_op jit(solution)/shard_map/all_to_all | solution.py:239
  46.5 0.1 multiply_reduce_fusion
  46.6 0.1 copy.10
  46.7 1.3 %shard_map.102 = bf16[4,128,256]{2,1,0:T(8,128)(2,1)S(1)} custom-call(s32[8,4]{1,0:T(8,128)S(1)} %convert_add_fusion.slots_ref, bf16[8,136,256]{2,1,0:T(8,128)(2,1)S(1)} %all-to-all-done.arrived_ref, bf16[16,256,256]{2,1,0:T(8,128)(2,1)S(1)} %bitcast.10), custom_call_target="tpu_custom_call" | custom-call | flops 536870912 | bytes 2916352 | tf_op jit(solution)/shard_map/pallas_call | solution.py:157
  48.1 15.1 %all_to_all.10 = bf16[4,128,256]{2,1,0:T(8,128)(2,1)S(1)} all-to-all(bf16[4,128,256]{2,1,0:T(8,128)(2,1)S(1)} %shard_map.102), channel_id=1, replica_groups={{4,6,0,2},{5,7,1,3},{12,14,8,10},{13,15,9,11},{20,22,16,18},{21,23,17,1..., dimensions={0} | all-to-all | bytes 524288 | tf_op jit(solution)/shard_map/all_to_all | solution.py:247
  63.1 0.7 %convert_reduce_fusion = f32[128,256]{1,0:T(8,128)} fusion(bf16[4,128,256]{2,1,0:T(8,128)(2,1)S(1)} %all_to_all.10), kind=kLoop, calls=%fused_computation.2 | loop fusion | flops 229376 | bytes 393216 | tf_op jit(solution)/shard_map/reduce_sum | solution.py:248
  (16 shorter events, 0.3 us)
Async XLA Ops:
  0.6 8.5 %copy-start.1 = (s32[32]{0:T(128)S(1)}, s32[32]{0:T(128)}, u32[]{:S(2)}) copy-start(s32[32]{0:T(128)} %param.14) | copy-start | bytes 388
  0.6 8.5 %copy-start.2 = (s32[1,16]{1,0:T(1,128)S(1)}, s32[1,16]{1,0:T(1,128)}, u32[]{:S(2)}) copy-start(s32[1,16]{1,0:T(1,128)} %param.13) | copy-start | bytes 196
  0.7 4.8 %collective-permute-start.1 = (f32[256,256]{1,0:T(8,128)}, f32[256,256]{1,0:T(8,128)S(1)}, u32[]{:S(2)}, u32[]{:S(2)}) collective-permute-start(f32[256,256]{1,0:T(8,128)} %bitcast.11), channel_id=1, source_target_pairs={{0,32},{64,96},{128,160},{192,224},{256,288},{320,352},{384,416},{... | collective-permute-start | bytes 786440 | tf_op jit(solution)/shard_map/ppermute | solution.py:179
  2.1 3.4 %collective-permute-start = (f32[128,128]{1,0:T(8,128)}, f32[128,128]{1,0:T(8,128)S(1)}, u32[]{:S(2)}, u32[]{:S(2)}) collective-permute-start(f32[128,128]{1,0:T(8,128)} %bitcast.15), channel_id=1, source_target_pairs={{0,32},{64,96},{128,160},{192,224},{256,288},{320,352},{384,416},{... | collective-permute-start | bytes 196616 | tf_op jit(solution)/shard_map/ppermute | solution.py:179
  6.1 7.8 %collective-permute-start.2 = (f32[320,256]{1,0:T(8,128)S(1)}, f32[320,256]{1,0:T(8,128)S(1)}, u32[]{:S(2)}, u32[]{:S(2)}) collective-permute-start(f32[320,256]{1,0:T(8,128)S(1)} %get-tuple-element.10.later_ref.operator_ref), channel_id=1, source_target_pairs={{160,224},{288,352},{416,480},{161,225},{289,353},{417,481},{162,2... | collective-permute-start | bytes 983048 | tf_op jit(solution)/shard_map/ppermute | solution.py:179
  7.4 0.7 %collective-permute-start.4 = (f32[128,256]{1,0:T(8,128)S(1)}, f32[128,256]{1,0:T(8,128)S(1)}, u32[]{:S(2)}, u32[]{:S(2)}) collective-permute-start(f32[128,256]{1,0:T(8,128)S(1)} %get-tuple-element.12), channel_id=1, source_target_pairs={{32,96},{33,97},{34,98},{35,99},{36,100},{37,101},{38,102},{39,103... | collective-permute-start | bytes 393224 | tf_op jit(solution)/shard_map/ppermute | solution.py:179
  8.5 5.7 %collective-permute-start.5 = (f32[128,256]{1,0:T(8,128)S(1)}, f32[128,256]{1,0:T(8,128)S(1)}, u32[]{:S(2)}, u32[]{:S(2)}) collective-permute-start(f32[128,256]{1,0:T(8,128)S(1)} %shard_map.98), channel_id=1, source_target_pairs={{96,224},{97,225},{98,226},{99,227},{100,228},{101,229},{102,230},... | collective-permute-start | bytes 393224 | tf_op jit(solution)/shard_map/ppermute | solution.py:179
  14.6 2.9 %collective-permute-start.6 = (f32[128,256]{1,0:T(8,128)S(1)}, f32[128,256]{1,0:T(8,128)S(1)}, u32[]{:S(2)}, u32[]{:S(2)}) collective-permute-start(f32[128,256]{1,0:T(8,128)S(1)} %shard_map.99), channel_id=1, source_target_pairs={{224,352},{225,353},{226,354},{227,355},{228,356},{229,357},{230,3... | collective-permute-start | bytes 393224 | tf_op jit(solution)/shard_map/ppermute | solution.py:179
  15.3 3.9 %collective-permute-start.9 = (f32[128,256]{1,0:T(8,128)S(1)}, f32[128,256]{1,0:T(8,128)S(1)}, u32[]{:S(2)}, u32[]{:S(2)}) collective-permute-start(f32[128,256]{1,0:T(8,128)S(1)} %broadcast_select_fusion.3), channel_id=1, source_target_pairs={{96,160},{224,288},{97,161},{225,289},{98,162},{226,290},{99,163},... | collective-permute-start | bytes 393224 | tf_op jit(solution)/shard_map/ppermute | solution.py:179
  16.2 5.3 %collective-permute-start.3 = (f32[320,256]{1,0:T(8,128)S(1)}, f32[320,256]{1,0:T(8,128)S(1)}, u32[]{:S(2)}, u32[]{:S(2)}) collective-permute-start(f32[320,256]{1,0:T(8,128)S(1)} %collective-permute-done.2.earlier_ref), channel_id=1, source_target_pairs={{224,192},{352,320},{480,448},{225,193},{353,321},{481,449},{226,1... | collective-permute-start | bytes 983048 | tf_op jit(solution)/shard_map/ppermute | solution.py:179
  17.9 2.1 %collective-permute-start.7 = (f32[128,256]{1,0:T(8,128)S(1)}, f32[128,256]{1,0:T(8,128)S(1)}, u32[]{:S(2)}, u32[]{:S(2)}) collective-permute-start(f32[128,256]{1,0:T(8,128)S(1)} %get-tuple-element.13), channel_id=1, source_target_pairs={{352,384},{353,385},{354,386},{355,387},{356,388},{357,389},{358,3... | collective-permute-start | bytes 393224 | tf_op jit(solution)/shard_map/ppermute | solution.py:179
  18.6 1.5 %collective-permute-start.8 = (f32[128,256]{1,0:T(8,128)S(1)}, f32[128,256]{1,0:T(8,128)S(1)}, u32[]{:S(2)}, u32[]{:S(2)}) collective-permute-start(f32[128,256]{1,0:T(8,128)S(1)} %get-tuple-element.14), channel_id=1, source_target_pairs={{352,448},{353,449},{354,450},{355,451},{356,452},{357,453},{358,4... | collective-permute-start | bytes 393224 | tf_op jit(solution)/shard_map/ppermute | solution.py:179
  19.3 0.8 %collective-permute-start.10 = (f32[128,256]{1,0:T(8,128)S(1)}, f32[128,256]{1,0:T(8,128)S(1)}, u32[]{:S(2)}, u32[]{:S(2)}) collective-permute-start(f32[128,256]{1,0:T(8,128)S(1)} %select_select_fusion.1), channel_id=1, source_target_pairs={{96,64},{160,128},{224,192},{288,256},{352,320},{97,65},{161,129},... | collective-permute-start | bytes 393224 | tf_op jit(solution)/shard_map/ppermute | solution.py:179
  20.1 10.9 %collective-permute-start.11 = (f32[128,256]{1,0:T(8,128)S(1)}, f32[128,256]{1,0:T(8,128)S(1)}, u32[]{:S(2)}, u32[]{:S(2)}) collective-permute-start(f32[128,256]{1,0:T(8,128)S(1)} %select_select_fusion), channel_id=1, source_target_pairs={{384,416},{448,480},{385,417},{449,481},{386,418},{450,482},{387,4... | collective-permute-start | bytes 393224 | tf_op jit(solution)/shard_map/ppermute | solution.py:179
  21.5 17.0 %copy-start.3 = (s32[4]{0:T(128)S(1)}, s32[4]{0:T(128)}, u32[]{:S(2)}) copy-start(s32[4]{0:T(128)} %constant.88) | copy-start | bytes 52
  21.5 25.2 %copy-start = (bf16[1,16,256,256]{3,2,1,0:T(8,128)(2,1)S(1)}, bf16[1,16,256,256]{3,2,1,0:T(8,128)(2,1)}, u32[]{:S(2)}) copy-start(bf16[1,16,256,256]{3,2,1,0:T(8,128)(2,1)} %param.11) | copy-start | bytes 6291460
  32.3 14.2 %all-to-all-start = ((bf16[8,136,256]{2,1,0:T(8,128)(2,1)}), bf16[8,136,256]{2,1,0:T(8,128)(2,1)S(1)}, u32[]{:S(2)}, u32[]{:S(2)}) async-start(bf16[8,136,256]{2,1,0:T(8,128)(2,1)} %get-tuple-element.17), calls=%async_computation | async-start | bytes 1114112 | tf_op jit(solution)/shard_map/all_to_all | solution.py:239

commit v4 on v3

--- a/solution.py
+++ b/solution.py
@@ -139,16 +139,21 @@
     slot_count, inner, columns = weights.shape
     rows = arrived.shape[1] - EXTRA
 
-    def kernel(slots_ref, arrived_ref, weights_ref, sums_ref):
+    def kernel(slots_ref, arrived_ref, weights_ref, sums_ref, total_ref):
         def one_target(target, carried):
-            total = jnp.zeros((rows, columns), jnp.float32)
+            total_ref[target] = jnp.zeros((rows, columns), jnp.float32)
             for source in range(sources):
                 slot = slots_ref[source, target]
-                block = arrived_ref[source, :rows, :]
-                block = jnp.where(slot >= 0, block, jnp.zeros_like(block))
-                slot = jnp.minimum(jnp.maximum(slot, 0), slot_count - 1)
-                total += jnp.dot(block, weights_ref[slot], preferred_element_type=jnp.float32)
-            sums_ref[target] = total.astype(jnp.bfloat16)
+
+                @pl.when(slot >= 0)
+                def _add(source=source, slot=slot):
+                    total_ref[target] += jnp.dot(
+                        arrived_ref[source, :rows, :],
+                        weights_ref[jnp.minimum(slot, slot_count - 1)],
+                        preferred_element_type=jnp.float32,
+                    )
+
+            sums_ref[target] = total_ref[target].astype(jnp.bfloat16)
             return carried
 
         for target in range(targets):
@@ -159,6 +164,7 @@
         out_shape=jax.ShapeDtypeStruct((targets, rows, columns), jnp.bfloat16),
         in_specs=[whole(pltpu.SMEM), whole(pltpu.VMEM), whole(pltpu.VMEM)],
         out_specs=whole(pltpu.VMEM),
+        scratch_shapes=[pltpu.VMEM((targets, rows, columns), jnp.float32)],
         compiler_params=pltpu.CompilerParams(vmem_limit_bytes=VMEM_GRANT),
         cost_estimate=pl.CostEstimate(
             flops=2 * sources * targets * rows * inner * columns,

time: 64.2 us -> 65.8 us (1.025)
  the two profiles are of different devices: /device:TPU:449 before, /device:TPU:510 now
where the time goes in v4:
time: 65.8 us; the launch traced here: 65.4 us
  waiting for transfers between devices  22.8 us (35%)
  starting transfers between devices  16.8 us (26%)
  blocking collectives  14.6 us (22%)
  Pallas kernels  7.02 us (11%)
  other arithmetic  2.46 us (4%)
  between operations  1.67 us (3%)
    all_to_all x1, blocking collectives, on_device(): lax.all_to_all(sums, 'sector', 0, 0, axis_index_groups=lines, tiled=True)  14.6 us
    ppermute x12, waiting for transfers between devices, sent(): return lax.ppermute(value, 'row', pairs)  13.1 us
    ppermute x12, starting transfers between devices, sent(): return lax.ppermute(value, 'row', pairs)  11.8 us
    all_to_all x1, waiting for transfers between devices, on_device(): lax.all_to_all(outgoing, 'sector', 0, 0, axis_index_groups=tiles, tiled=T...  9.71 us
    all_to_all x1, starting transfers between devices, on_device(): lax.all_to_all(outgoing, 'sector', 0, 0, axis_index_groups=tiles, tiled=T...  5.06 us
    pallas_call x7, Pallas kernels, on_core(): pl.pallas_call(kernel, out_shape=shapes, in_specs=[whole(space) for space...  3.72 us
    pallas_call x1, Pallas kernels, environment_sums(): pl.pallas_call(kernel, out_shape=jax.ShapeDtypeStruct((targets, rows, col...  3.31 us
  transfers between devices with their start and end apart: 13, of which 3 were waited for; matrix products, arithmetic and copies ran while one was open for 3% of the time, Pallas kernels for 2%

profile of v4, /device:TPU:510, one launch (start us, length us, event | category | flops | bytes accessed | tf_op | source)
XLA Modules:
  0.0 65.4 jit_solution(17137298109299870543)
XLA Ops:
  0.6 0.0 copy-start.1
  0.7 1.9 %collective-permute-start.1 = (f32[256,256]{1,0:T(8,128)}, f32[256,256]{1,0:T(8,128)S(1)}, u32[]{:S(2)}, u32[]{:S(2)}) collective-permute-start(f32[256,256]{1,0:T(8,128)} %bitcast.11), channel_id=1, source_target_pairs={{0,32},{64,96},{128,160},{192,224},{256,288},{320,352},{384,416},{... | collective-permute-start | bytes 786440 | tf_op jit(solution)/shard_map/ppermute | solution.py:185
  2.5 1.3 %collective-permute-start = (f32[128,128]{1,0:T(8,128)}, f32[128,128]{1,0:T(8,128)S(1)}, u32[]{:S(2)}, u32[]{:S(2)}) collective-permute-start(f32[128,128]{1,0:T(8,128)} %bitcast.15), channel_id=1, source_target_pairs={{0,32},{64,96},{128,160},{192,224},{256,288},{320,352},{384,416},{... | collective-permute-start | bytes 196616 | tf_op jit(solution)/shard_map/ppermute | solution.py:185
  4.5 1.1 %select_maximum_fusion.stacked_ref = f32[512,256]{1,0:T(8,128)S(1)} fusion(f32[128,128]{1,0:T(8,128)} %bitcast.16, f32[256,256]{1,0:T(8,128)} %bitcast.12, f32[128,256]{1,0:T(8,128)} %bitcast.13), kind=kLoop, calls=%fused_computation | loop fusion | flops 524288 | bytes 983040 | tf_op jit(solution)/shard_map/concatenate | solution.py:191
  5.6 0.0 collective-permute-done.left_low_ref
  5.6 0.0 collective-permute-done.1.right_low_ref
  5.6 0.6 shard_map.95
  6.2 0.7 %collective-permute-start.2 = (f32[320,256]{1,0:T(8,128)S(1)}, f32[320,256]{1,0:T(8,128)S(1)}, u32[]{:S(2)}, u32[]{:S(2)}) collective-permute-start(f32[320,256]{1,0:T(8,128)S(1)} %get-tuple-element.10.later_ref.operator_ref), channel_id=1, source_target_pairs={{160,224},{288,352},{416,480},{161,225},{289,353},{417,481},{162,2... | collective-permute-start | bytes 983048 | tf_op jit(solution)/shard_map/ppermute | solution.py:185
  6.9 0.7 %collective-permute-start.4 = (f32[128,256]{1,0:T(8,128)S(1)}, f32[128,256]{1,0:T(8,128)S(1)}, u32[]{:S(2)}, u32[]{:S(2)}) collective-permute-start(f32[128,256]{1,0:T(8,128)S(1)} %get-tuple-element.12), channel_id=1, source_target_pairs={{32,96},{33,97},{34,98},{35,99},{36,100},{37,101},{38,102},{39,103... | collective-permute-start | bytes 393224 | tf_op jit(solution)/shard_map/ppermute | solution.py:185
  7.6 0.0 collective-permute-done.4.block_ref
  7.6 0.4 shard_map.98
  8.0 0.7 %collective-permute-start.5 = (f32[128,256]{1,0:T(8,128)S(1)}, f32[128,256]{1,0:T(8,128)S(1)}, u32[]{:S(2)}, u32[]{:S(2)}) collective-permute-start(f32[128,256]{1,0:T(8,128)S(1)} %shard_map.98), channel_id=1, source_target_pairs={{96,224},{97,225},{98,226},{99,227},{100,228},{101,229},{102,230},... | collective-permute-start | bytes 393224 | tf_op jit(solution)/shard_map/ppermute | solution.py:185
  8.7 0.0 copy-done.1
  8.7 0.0 copy-done.2
  8.7 0.2 select_reduce_fusion.1
  8.9 0.0 collective-permute-done.2.earlier_ref
  8.9 0.3 shard_map.97.operator_ref
  9.2 0.0 collective-permute-done.5.block_ref
  9.2 0.4 shard_map.99
  9.6 0.7 %collective-permute-start.6 = (f32[128,256]{1,0:T(8,128)S(1)}, f32[128,256]{1,0:T(8,128)S(1)}, u32[]{:S(2)}, u32[]{:S(2)}) collective-permute-start(f32[128,256]{1,0:T(8,128)S(1)} %shard_map.99), channel_id=1, source_target_pairs={{224,352},{225,353},{226,354},{227,355},{228,356},{229,357},{230,3... | collective-permute-start | bytes 393224 | tf_op jit(solution)/shard_map/ppermute | solution.py:185
  10.3 0.7 %collective-permute-start.9 = (f32[128,256]{1,0:T(8,128)S(1)}, f32[128,256]{1,0:T(8,128)S(1)}, u32[]{:S(2)}, u32[]{:S(2)}) collective-permute-start(f32[128,256]{1,0:T(8,128)S(1)} %broadcast_select_fusion.3), channel_id=1, source_target_pairs={{96,160},{224,288},{97,161},{225,289},{98,162},{226,290},{99,163},... | collective-permute-start | bytes 393224 | tf_op jit(solution)/shard_map/ppermute | solution.py:185
  11.1 0.1 select_reduce_fusion
  11.2 1.3 %collective-permute-start.3 = (f32[320,256]{1,0:T(8,128)S(1)}, f32[320,256]{1,0:T(8,128)S(1)}, u32[]{:S(2)}, u32[]{:S(2)}) collective-permute-start(f32[320,256]{1,0:T(8,128)S(1)} %collective-permute-done.2.earlier_ref), channel_id=1, source_target_pairs={{224,192},{352,320},{480,448},{225,193},{353,321},{481,449},{226,1... | collective-permute-start | bytes 983048 | tf_op jit(solution)/shard_map/ppermute | solution.py:185
  12.5 0.0 collective-permute-done.6.block_ref
  12.5 0.4 shard_map.100
  12.9 0.7 %collective-permute-start.7 = (f32[128,256]{1,0:T(8,128)S(1)}, f32[128,256]{1,0:T(8,128)S(1)}, u32[]{:S(2)}, u32[]{:S(2)}) collective-permute-start(f32[128,256]{1,0:T(8,128)S(1)} %get-tuple-element.13), channel_id=1, source_target_pairs={{352,384},{353,385},{354,386},{355,387},{356,388},{357,389},{358,3... | collective-permute-start | bytes 393224 | tf_op jit(solution)/shard_map/ppermute | solution.py:185
  13.6 1.3 %collective-permute-start.8 = (f32[128,256]{1,0:T(8,128)S(1)}, f32[128,256]{1,0:T(8,128)S(1)}, u32[]{:S(2)}, u32[]{:S(2)}) collective-permute-start(f32[128,256]{1,0:T(8,128)S(1)} %get-tuple-element.14), channel_id=1, source_target_pairs={{352,448},{353,449},{354,450},{355,451},{356,452},{357,453},{358,4... | collective-permute-start | bytes 393224 | tf_op jit(solution)/shard_map/ppermute | solution.py:185
  14.9 0.0 collective-permute-done.9
  14.9 0.7 %collective-permute-start.10 = (f32[128,256]{1,0:T(8,128)S(1)}, f32[128,256]{1,0:T(8,128)S(1)}, u32[]{:S(2)}, u32[]{:S(2)}) collective-permute-start(f32[128,256]{1,0:T(8,128)S(1)} %select_select_fusion.1), channel_id=1, source_target_pairs={{96,64},{160,128},{224,192},{288,256},{352,320},{97,65},{161,129},... | collective-permute-start | bytes 393224 | tf_op jit(solution)/shard_map/ppermute | solution.py:185
  15.7 0.0 collective-permute-done.7
  15.7 12.5 %collective-permute-done.8 = f32[128,256]{1,0:T(8,128)S(1)} collective-permute-done((f32[128,256]{1,0:T(8,128)S(1)}, f32[128,256]{1,0:T(8,128)S(1)}, u32[]{:S(2)}, u32[]{:S(2)}) %collective-permute-start.8) | collective-permute-done | bytes 131104 | tf_op jit(solution)/shard_map/ppermute | solution.py:185
  28.2 0.0 collective-permute-done.10
  28.2 1.3 %collective-permute-start.11 = (f32[128,256]{1,0:T(8,128)S(1)}, f32[128,256]{1,0:T(8,128)S(1)}, u32[]{:S(2)}, u32[]{:S(2)}) collective-permute-start(f32[128,256]{1,0:T(8,128)S(1)} %select_select_fusion), channel_id=1, source_target_pairs={{384,416},{448,480},{385,417},{449,481},{386,418},{450,482},{387,4... | collective-permute-start | bytes 393224 | tf_op jit(solution)/shard_map/ppermute | solution.py:185
  29.5 0.0 collective-permute-done.3
  29.6 0.0 copy-start.3
  29.6 0.0 copy-start
  29.6 0.3 shard_map.96
  30.0 0.5 collective-permute-done.11
  30.5 1.3 %shard_map.101 = (f32[128,256]{1,0:T(8,128)}, bf16[8,136,256]{2,1,0:T(8,128)(2,1)}) custom-call(f32[320,256]{1,0:T(8,128)S(1)} %broadcast_select_fusion.2.operator_ref, f32[128,256]{1,0:T(8,128)S(1)} %broadcast_select_fusion.4.block_ref, bf16[8,256]{1,0:T(8,128)(2,1)S(1)} %broadcast_in_dim.6.extra_ref), custom_call_target="tpu_custom_call" | custom-call | flops 119537664 | bytes 933888 | tf_op jit(solution)/shard_map/pallas_call | solution.py:56
  31.8 5.1 %all-to-all-start = ((bf16[8,136,256]{2,1,0:T(8,128)(2,1)}), bf16[8,136,256]{2,1,0:T(8,128)(2,1)S(1)}, u32[]{:S(2)}, u32[]{:S(2)}) async-start(bf16[8,136,256]{2,1,0:T(8,128)(2,1)} %get-tuple-element.17), calls=%async_computation | async-start | bytes 1114112 | tf_op jit(solution)/shard_map/all_to_all | solution.py:245
  36.9 0.1 fusion
  36.9 9.7 %all-to-all-done.arrived_ref = bf16[8,136,256]{2,1,0:T(8,128)(2,1)S(1)} async-done(((bf16[8,136,256]{2,1,0:T(8,128)(2,1)}), bf16[8,136,256]{2,1,0:T(8,128)(2,1)S(1)}, u32[]{:S(2)}, u32[]{:S(2)}) %all-to-all-start) | async-done | bytes 557088 | tf_op jit(solution)/shard_map/all_to_all | solution.py:245
  46.7 0.1 multiply_reduce_fusion
  46.8 0.1 copy.10
  46.8 0.0 copy-done
  46.8 3.3 %shard_map.102 = bf16[4,128,256]{2,1,0:T(8,128)(2,1)S(1)} custom-call(s32[8,4]{1,0:T(8,128)S(1)} %convert_add_fusion.slots_ref, bf16[8,136,256]{2,1,0:T(8,128)(2,1)S(1)} %all-to-all-done.arrived_ref, bf16[16,256,256]{2,1,0:T(8,128)(2,1)S(1)} %bitcast.10), custom_call_target="tpu_custom_call" | custom-call | flops 536870912 | bytes 2916352 | tf_op jit(solution)/shard_map/pallas_call | solution.py:162
  50.2 14.6 %all_to_all.10 = bf16[4,128,256]{2,1,0:T(8,128)(2,1)S(1)} all-to-all(bf16[4,128,256]{2,1,0:T(8,128)(2,1)S(1)} %shard_map.102), channel_id=1, replica_groups={{4,6,0,2},{5,7,1,3},{12,14,8,10},{13,15,9,11},{20,22,16,18},{21,23,17,1..., dimensions={0} | all-to-all | bytes 524288 | tf_op jit(solution)/shard_map/all_to_all | solution.py:253
  64.7 0.7 %convert_reduce_fusion = f32[128,256]{1,0:T(8,128)} fusion(bf16[4,128,256]{2,1,0:T(8,128)(2,1)S(1)} %all_to_all.10), kind=kLoop, calls=%fused_computation.2 | loop fusion | flops 229376 | bytes 393216 | tf_op jit(solution)/shard_map/reduce_sum | solution.py:254
  (16 shorter events, 0.3 us)
Async XLA Ops:
  0.6 8.0 %copy-start.1 = (s32[32]{0:T(128)S(1)}, s32[32]{0:T(128)}, u32[]{:S(2)}) copy-start(s32[32]{0:T(128)} %param.14) | copy-start | bytes 388
  0.6 8.0 %copy-start.2 = (s32[1,16]{1,0:T(1,128)S(1)}, s32[1,16]{1,0:T(1,128)}, u32[]{:S(2)}) copy-start(s32[1,16]{1,0:T(1,128)} %param.13) | copy-start | bytes 196
  0.7 4.9 %collective-permute-start.1 = (f32[256,256]{1,0:T(8,128)}, f32[256,256]{1,0:T(8,128)S(1)}, u32[]{:S(2)}, u32[]{:S(2)}) collective-permute-start(f32[256,256]{1,0:T(8,128)} %bitcast.11), channel_id=1, source_target_pairs={{0,32},{64,96},{128,160},{192,224},{256,288},{320,352},{384,416},{... | collective-permute-start | bytes 786440 | tf_op jit(solution)/shard_map/ppermute | solution.py:185
  2.5 3.0 %collective-permute-start = (f32[128,128]{1,0:T(8,128)}, f32[128,128]{1,0:T(8,128)S(1)}, u32[]{:S(2)}, u32[]{:S(2)}) collective-permute-start(f32[128,128]{1,0:T(8,128)} %bitcast.15), channel_id=1, source_target_pairs={{0,32},{64,96},{128,160},{192,224},{256,288},{320,352},{384,416},{... | collective-permute-start | bytes 196616 | tf_op jit(solution)/shard_map/ppermute | solution.py:185
  6.2 2.7 %collective-permute-start.2 = (f32[320,256]{1,0:T(8,128)S(1)}, f32[320,256]{1,0:T(8,128)S(1)}, u32[]{:S(2)}, u32[]{:S(2)}) collective-permute-start(f32[320,256]{1,0:T(8,128)S(1)} %get-tuple-element.10.later_ref.operator_ref), channel_id=1, source_target_pairs={{160,224},{288,352},{416,480},{161,225},{289,353},{417,481},{162,2... | collective-permute-start | bytes 983048 | tf_op jit(solution)/shard_map/ppermute | solution.py:185
  6.9 0.7 %collective-permute-start.4 = (f32[128,256]{1,0:T(8,128)S(1)}, f32[128,256]{1,0:T(8,128)S(1)}, u32[]{:S(2)}, u32[]{:S(2)}) collective-permute-start(f32[128,256]{1,0:T(8,128)S(1)} %get-tuple-element.12), channel_id=1, source_target_pairs={{32,96},{33,97},{34,98},{35,99},{36,100},{37,101},{38,102},{39,103... | collective-permute-start | bytes 393224 | tf_op jit(solution)/shard_map/ppermute | solution.py:185
  8.0 1.2 %collective-permute-start.5 = (f32[128,256]{1,0:T(8,128)S(1)}, f32[128,256]{1,0:T(8,128)S(1)}, u32[]{:S(2)}, u32[]{:S(2)}) collective-permute-start(f32[128,256]{1,0:T(8,128)S(1)} %shard_map.98), channel_id=1, source_target_pairs={{96,224},{97,225},{98,226},{99,227},{100,228},{101,229},{102,230},... | collective-permute-start | bytes 393224 | tf_op jit(solution)/shard_map/ppermute | solution.py:185
  9.6 2.8 %collective-permute-start.6 = (f32[128,256]{1,0:T(8,128)S(1)}, f32[128,256]{1,0:T(8,128)S(1)}, u32[]{:S(2)}, u32[]{:S(2)}) collective-permute-start(f32[128,256]{1,0:T(8,128)S(1)} %shard_map.99), channel_id=1, source_target_pairs={{224,352},{225,353},{226,354},{227,355},{228,356},{229,357},{230,3... | collective-permute-start | bytes 393224 | tf_op jit(solution)/shard_map/ppermute | solution.py:185
  10.3 4.5 %collective-permute-start.9 = (f32[128,256]{1,0:T(8,128)S(1)}, f32[128,256]{1,0:T(8,128)S(1)}, u32[]{:S(2)}, u32[]{:S(2)}) collective-permute-start(f32[128,256]{1,0:T(8,128)S(1)} %broadcast_select_fusion.3), channel_id=1, source_target_pairs={{96,160},{224,288},{97,161},{225,289},{98,162},{226,290},{99,163},... | collective-permute-start | bytes 393224 | tf_op jit(solution)/shard_map/ppermute | solution.py:185
  11.2 18.4 %collective-permute-start.3 = (f32[320,256]{1,0:T(8,128)S(1)}, f32[320,256]{1,0:T(8,128)S(1)}, u32[]{:S(2)}, u32[]{:S(2)}) collective-permute-start(f32[320,256]{1,0:T(8,128)S(1)} %collective-permute-done.2.earlier_ref), channel_id=1, source_target_pairs={{224,192},{352,320},{480,448},{225,193},{353,321},{481,449},{226,1... | collective-permute-start | bytes 983048 | tf_op jit(solution)/shard_map/ppermute | solution.py:185
  12.9 2.8 %collective-permute-start.7 = (f32[128,256]{1,0:T(8,128)S(1)}, f32[128,256]{1,0:T(8,128)S(1)}, u32[]{:S(2)}, u32[]{:S(2)}) collective-permute-start(f32[128,256]{1,0:T(8,128)S(1)} %get-tuple-element.13), channel_id=1, source_target_pairs={{352,384},{353,385},{354,386},{355,387},{356,388},{357,389},{358,3... | collective-permute-start | bytes 393224 | tf_op jit(solution)/shard_map/ppermute | solution.py:185
  13.6 14.6 %collective-permute-start.8 = (f32[128,256]{1,0:T(8,128)S(1)}, f32[128,256]{1,0:T(8,128)S(1)}, u32[]{:S(2)}, u32[]{:S(2)}) collective-permute-start(f32[128,256]{1,0:T(8,128)S(1)} %get-tuple-element.14), channel_id=1, source_target_pairs={{352,448},{353,449},{354,450},{355,451},{356,452},{357,453},{358,4... | collective-permute-start | bytes 393224 | tf_op jit(solution)/shard_map/ppermute | solution.py:185
  14.9 13.3 %collective-permute-start.10 = (f32[128,256]{1,0:T(8,128)S(1)}, f32[128,256]{1,0:T(8,128)S(1)}, u32[]{:S(2)}, u32[]{:S(2)}) collective-permute-start(f32[128,256]{1,0:T(8,128)S(1)} %select_select_fusion.1), channel_id=1, source_target_pairs={{96,64},{160,128},{224,192},{288,256},{352,320},{97,65},{161,129},... | collective-permute-start | bytes 393224 | tf_op jit(solution)/shard_map/ppermute | solution.py:185
  28.2 2.3 %collective-permute-start.11 = (f32[128,256]{1,0:T(8,128)S(1)}, f32[128,256]{1,0:T(8,128)S(1)}, u32[]{:S(2)}, u32[]{:S(2)}) collective-permute-start(f32[128,256]{1,0:T(8,128)S(1)} %select_select_fusion), channel_id=1, source_target_pairs={{384,416},{448,480},{385,417},{449,481},{386,418},{450,482},{387,4... | collective-permute-start | bytes 393224 | tf_op jit(solution)/shard_map/ppermute | solution.py:185
  29.6 7.3 %copy-start.3 = (s32[4]{0:T(128)S(1)}, s32[4]{0:T(128)}, u32[]{:S(2)}) copy-start(s32[4]{0:T(128)} %constant.88) | copy-start | bytes 52
  29.6 17.2 %copy-start = (bf16[1,16,256,256]{3,2,1,0:T(8,128)(2,1)S(1)}, bf16[1,16,256,256]{3,2,1,0:T(8,128)(2,1)}, u32[]{:S(2)}) copy-start(bf16[1,16,256,256]{3,2,1,0:T(8,128)(2,1)} %param.11) | copy-start | bytes 6291460
  31.8 14.8 %all-to-all-start = ((bf16[8,136,256]{2,1,0:T(8,128)(2,1)}), bf16[8,136,256]{2,1,0:T(8,128)(2,1)S(1)}, u32[]{:S(2)}, u32[]{:S(2)}) async-start(bf16[8,136,256]{2,1,0:T(8,128)(2,1)} %get-tuple-element.17), calls=%async_computation | async-start | bytes 1114112 | tf_op jit(solution)/shard_map/all_to_all | solution.py:245
